TPU v7x, 128 devices: a whole 4x4x4 slice. The times are simulated.
128 devices in a mesh: tile: 32 (over x_lo, z, y), cond: 4 (over x_hi, core).
Axes of the slice: x: 4 (x_hi: 2, x_lo: 2; x = x_hi * 2 + x_lo), y: 4, z: 4, core: 2. Of those that a mesh axis runs over, the one named last changes fastest.
Arguments:
- theta: float32 [16384, 512], P(('tile', 'cond')), may hold values from -6 to 6
- target: int32 [16384, 512], P('tile'), may hold values 0 or 1
- kernel_real: float32 [8, 2, 65, 65], P('cond'), may hold values from -24 to 24
- kernel_imag: float32 [8, 2, 65, 65], P('cond'), may hold values from -24 to 24
- weights: int32 [8], replicated, may hold values from 1 to 4
- thresholds: float32 [8], P('cond'), may hold values from 0.5 to 1.5
Outputs:
- gradient: float32 [16384, 512], P(('tile', 'cond'))
Inputs may be any that keep to these rules, and one draw needn't show every extreme that they name: Each pixel of the target is 0 or 1. Condition weights are small positive integers.
All inputs are finite; a program needn't handle non-finite values. No bound on the sum of `target` on one device may be relied on, other than what follows from the above.
Results may differ from a plain program's by a relative error of at most 0.00021.
Values sent between devices are 32-bit elements; how exact they have to be, the bound alone decides.
A program may use at most 64 MiB of HBM per device.

v0:
```python
import functools
import math

import jax
import jax.numpy as jnp
import ml_dtypes
import numpy as np
from jax import lax
from jax.experimental import pallas as pl
from jax.experimental.pallas import tpu as pltpu
from jax.sharding import PartitionSpec as P

TP = 512
HALO = 32
KSUP = 65
HALF = KSUP // 2
CONDS = 8
KERNELS = 2
SIZE = TP + 2 * HALO
ROWS = 128
GROUP = 4
LOCAL = CONDS // GROUP
UH = 40
UR = 2 * UH
VH = 64
VR = 2 * VH

MASK_STEEP = 2.0
RESIST_STEEP = 4.0
BAND_WEIGHT = 1.0

BF = jnp.bfloat16
F32 = jnp.float32
MESH = pl.DeviceIdType.MESH


def split(x):
    hi = x.astype(BF)
    return hi, (x - hi.astype(F32)).astype(BF)


def np_split(x):
    hi = x.astype(ml_dtypes.bfloat16)
    return hi, (x - hi.astype(np.float64)).astype(ml_dtypes.bfloat16)


def basis(positions, pitch):
    phase = (np.asarray(positions)[:, None] * np.arange(HALF + 1)[None, :]) % SIZE
    angles = phase * (2.0 * math.pi / SIZE)
    out = np.zeros((len(positions), 2 * pitch))
    out[:, : HALF + 1] = np.cos(angles)
    out[:, pitch : pitch + HALF + 1] = np.sin(angles)
    out[:, pitch] = 0.0
    return out


def parity(pitch, columns):
    out = np.zeros((2 * pitch, columns))
    out[0, HALF] = 1.0
    for j in range(1, HALF + 1):
        out[j, HALF + j] = 1.0
        out[j, HALF - j] = 1.0
        out[pitch + j, HALF + j] = 1.0
        out[pitch + j, HALF - j] = -1.0
    return out


def tables():
    bf = ml_dtypes.bfloat16
    cols = basis(np.arange(TP) + HALO, VH)
    hi, lo = np_split(cols)
    by = np.concatenate([hi, lo], axis=1)
    bt = np.concatenate([hi.T, hi.T, lo.T], axis=0)
    pack = []
    turned = []
    for c in range(GROUP):
        own = basis(np.arange(ROWS) + HALO + ROWS * c, UH)
        near = np.zeros_like(own)
        if c == 0:
            near[:HALO] = basis(np.arange(HALO) + HALO + TP, UH)
        if c == GROUP - 1:
            near[ROWS - HALO :] = basis(np.arange(HALO), UH)
        row = []
        column = []
        for table in (own, near):
            thi, tlo = np_split(table)
            row += [thi, tlo, thi, np.zeros((ROWS, 256 - 3 * UR), bf)]
            column.append(np.concatenate([thi.T, thi.T], axis=1))
            column.append(np.concatenate([tlo.T, np.zeros((UR, ROWS), bf)], axis=1))
        pack.append(np.concatenate(row, axis=1))
        turned.append(np.concatenate(column, axis=0))
    pv = parity(VH, VR).T.astype(bf)
    pv = np.concatenate([pv, pv], axis=0)
    pu = parity(UH, UR).astype(bf)
    pu = np.concatenate([pu, pu], axis=1)
    return by, bt, np.stack(pack), np.stack(turned), pv, pu


def dot(a, b):
    return jnp.dot(a, b, preferred_element_type=F32)


def kernel(
    tiles,
    theta_h, target_h, kr_h, ki_h, weights_s, thresholds_s, by_h, bt_h, pack_h, turned_h, pv_h, pu_h,
    out_h,
    theta_v, target_v, raw_v, by, bt, pack, turned, pv, pu,
    stack, zbuf, rown, rhalo, rin, rsum, aown, ain, anear, jbuf, amps, resists, band, grad_v,
    load_sem, zs_sem, zr_sem, rs_sem, rr_sem, hs_sem, hr_sem, as_sem, ar_sem, near_sem, out_sem,
):
    t = lax.axis_index("tile")
    c = lax.axis_index("cond")
    first = c == 0
    final = c == GROUP - 1
    has_prev = t > 0
    has_next = t < tiles - 1

    loads = []

    def load(src, dst):
        copy = pltpu.make_async_copy(src, dst, load_sem.at[len(loads)])
        copy.start()
        loads.append(copy)
        return copy

    load_kr = load(kr_h, raw_v.at[0])
    load_ki = load(ki_h, raw_v.at[1])
    load_pv = load(pv_h, pv)
    load_pu = load(pu_h, pu)
    load_theta = load(theta_h, theta_v)
    load_by = load(by_h, by)
    load_turned = load(turned_h.at[c], turned)
    load_pack = load(pack_h.at[c], pack)
    load_bt = load(bt_h, bt)
    load_target = load(target_h.at[pl.ds(pl.multiple_of(c * ROWS, ROWS), ROWS), :], target_v)

    def partner(mask):
        return (t, c ^ mask)

    barrier = pltpu.get_barrier_semaphore()

    def greet(device):
        pl.semaphore_signal(barrier, inc=1, device_id=device, device_id_type=MESH)

    for mask in range(1, GROUP):
        greet(partner(mask))
    for other in range(GROUP):
        @pl.when(has_next & (final | (other == 0)))
        def _(other=other):
            greet((t + 1, other))

        @pl.when(has_prev & (first | (other == GROUP - 1)))
        def _(other=other):
            greet((t - 1, other))

    stack[...] = jnp.zeros_like(stack)
    load_kr.wait()
    load_ki.wait()
    for ri in range(2):
        for l in range(LOCAL):
            for k in range(KERNELS):
                at = ((l * KERNELS + k) * 2 + ri) * UR
                stack[at : at + KSUP, 0:KSUP] = raw_v[ri, l, k]
    load_pv.wait()
    load_pu.wait()
    hi, lo = split(stack[...])
    folded = dot(jnp.concatenate([hi, lo], axis=1), pv[...])
    hi, lo = split(folded)
    for n in range(LOCAL * KERNELS * 2):
        rhs = jnp.concatenate([hi[n * UR : (n + 1) * UR], lo[n * UR : (n + 1) * UR]], axis=0)
        zbuf[0, n // 4, (n // 2) % 2, n % 2] = dot(pu[...], rhs)
    for l in range(LOCAL):
        zbuf[0, l, 0, 0, HALF + 2 : HALF + 3, :] = jnp.full((1, VR), thresholds_s[l], F32)

    load_theta.wait()
    load_by.wait()
    load_turned.wait()
    mask_rows = jnp.tanh(MASK_STEEP * theta_v[...])
    hi, lo = split(mask_rows)
    wide = dot(jnp.concatenate([hi, lo], axis=0), by[...])
    column = wide[:ROWS, :VR] + wide[:ROWS, VR:] + wide[ROWS:, :VR]
    hi, lo = split(column)
    both = dot(turned[...], jnp.concatenate([hi, lo], axis=0))
    rown[...] = both[:UR] + both[UR : 2 * UR]
    rhalo[...] = both[2 * UR : 3 * UR] + both[3 * UR :]

    across_next = jnp.where(final, GROUP, 1) * has_next.astype(jnp.int32)
    across_prev = jnp.where(first, GROUP, 1) * has_prev.astype(jnp.int32)
    pl.semaphore_wait(barrier, GROUP - 1 + across_next + across_prev)

    def remote(src, dst, send, recv, device):
        return pltpu.make_async_remote_copy(
            src_ref=src, dst_ref=dst, send_sem=send, recv_sem=recv, device_id=device, device_id_type=MESH
        )

    def halo_next(other):
        return remote(rhalo, rin.at[3], hs_sem.at[other], hr_sem.at[0], (t + 1, other))

    def halo_prev(other):
        return remote(rhalo, rin.at[4], hs_sem.at[other], hr_sem.at[1], (t - 1, other))

    def part(mask):
        return remote(rown, rin.at[mask - 1], rs_sem.at[mask - 1], rr_sem.at[mask - 1], partner(mask))

    def kernels_to(mask):
        return remote(zbuf.at[0], zbuf.at[mask], zs_sem.at[mask - 1], zr_sem.at[mask - 1], partner(mask))

    @pl.when(has_next & final)
    def _():
        for other in range(GROUP):
            halo_next(other).start()

    @pl.when(has_prev & first)
    def _():
        for other in range(GROUP):
            halo_prev(other).start()

    for mask in range(1, GROUP):
        part(mask).start()
    for mask in range(1, GROUP):
        kernels_to(mask).start()

    @pl.when(jnp.logical_not(has_prev))
    def _():
        rin[3] = jnp.zeros((UR, VR), F32)

    @pl.when(jnp.logical_not(has_next))
    def _():
        rin[4] = jnp.zeros((UR, VR), F32)

    @pl.when(has_prev)
    def _():
        halo_next(0).wait_recv()

    @pl.when(has_next)
    def _():
        halo_prev(0).wait_recv()

    for mask in range(1, GROUP):
        part(mask).wait_recv()

    lane = lax.broadcasted_iota(jnp.int32, (UH, VR), 1)
    low = lane < VH
    sign_v = jnp.where(low, 1.0, -1.0).astype(F32)

    def swap(x):
        return pltpu.roll(x, VH, 1)

    total = rown[...] + rin[0] + rin[1] + rin[2] + rin[3] + rin[4]
    total = total * (1.0 / (SIZE * SIZE))
    for h in range(2):
        here = total[h * UH : (h + 1) * UH]
        there = total[(1 - h) * UH : (2 - h) * UH]
        sign_u = 1.0 - 2.0 * h
        rsum[0, h] = here
        rsum[1, h] = sign_v * swap(here)
        rsum[2, h] = sign_u * there
        rsum[3, h] = (-sign_u) * sign_v * swap(there)

    def parts_of(s, l, k):
        out = []
        for ri in range(2):
            for h in range(2):
                z = zbuf[s, l, k, ri, h * UH : (h + 1) * UH, :]
                turn = swap(z)
                out.append(jnp.where(low, z, turn))
                out.append(jnp.where(low, turn, z))
        return out

    load_pack.wait()
    load_bt.wait()

    def forward(i, carry):
        s = i // LOCAL
        l = i % LOCAL

        @pl.when((l == 0) & (s > 0))
        def _():
            remote(zbuf.at[0], zbuf.at[s], zs_sem.at[s - 1], zr_sem.at[s - 1], (t, c ^ 1)).wait_recv()

        intensity = None
        for k in range(KERNELS):
            ee_r, eo_r, oe_r, oo_r, ee_i, eo_i, oe_i, oo_i = parts_of(s, l, k)
            real = []
            imag = []
            for h in range(2):
                r0, r1, r2, r3 = (rsum[n, h] for n in range(4))
                real.append(ee_r * r0 + eo_i * r1 + oe_i * r2 + oo_r * r3)
                imag.append(ee_i * r0 - eo_r * r1 - oe_r * r2 + oo_i * r3)
            grid = jnp.concatenate(
                [jnp.concatenate(real, axis=0), jnp.concatenate(imag, axis=0)], axis=1
            )
            hi, lo = split(grid)
            tall = dot(pack[:, : 3 * UR], jnp.concatenate([hi, hi, lo], axis=0))
            tall = jnp.concatenate([tall[:, :VR], tall[:, VR:]], axis=0)
            hi, lo = split(tall)
            amp = dot(jnp.concatenate([hi, lo, hi], axis=1), bt[...])
            amps[i, k] = amp
            power = amp[:ROWS] * amp[:ROWS] + amp[ROWS:] * amp[ROWS:]
            intensity = power if intensity is None else intensity + power
        level = zbuf[s, l, 0, 0, HALF + 2 : HALF + 3, 0:1]
        resist = jax.nn.sigmoid(RESIST_STEEP * (intensity - level))
        resists[i] = resist

        @pl.when(i == 0)
        def _():
            band[...] = resist

        @pl.when(i > 0)
        def _():
            band[...] += resist

        return carry

    lax.fori_loop(0, CONDS, forward, 0)

    load_target.wait()
    weight_sum = weights_s[0]
    for n in range(1, CONDS):
        weight_sum = weight_sum + weights_s[n]
    weight_sum = jnp.full((8, TP), weight_sum, jnp.int32).astype(F32)
    jbuf[...] = jnp.zeros_like(jbuf)

    def backward(i, carry):
        s = i // LOCAL
        l = i % LOCAL
        weight = jnp.full((8, TP), weights_s[(c ^ s) * LOCAL + l], jnp.int32).astype(F32) / weight_sum
        weight = weight[0:1]
        resist = resists[i]
        slope = 2.0 * weight * (resist - target_v[...].astype(F32)) + (2.0 * BAND_WEIGHT / CONDS) * (
            resist - band[...] * (1.0 / CONDS)
        )
        field = 2.0 * slope * RESIST_STEEP * resist * (1.0 - resist)
        field = jnp.concatenate([field, field], axis=0)
        for k in range(KERNELS):
            hi, lo = split(field * amps[i, k])
            wide = dot(jnp.concatenate([hi, lo], axis=0), by[...])
            drive = wide[: 2 * ROWS, :VR] + wide[: 2 * ROWS, VR:] + wide[2 * ROWS :, :VR]
            drive = jnp.concatenate([drive[:ROWS], drive[ROWS:]], axis=1)
            hi, lo = split(drive)
            back = dot(turned[: 2 * UR, :], jnp.concatenate([hi, lo], axis=0))
            back = back[:UR] + back[UR:]
            ee_r, eo_r, oe_r, oo_r, ee_i, eo_i, oe_i, oo_i = parts_of(s, l, k)
            for h in range(2):
                qr = back[h * UH : (h + 1) * UH, :VR]
                qi = back[h * UH : (h + 1) * UH, VR:]
                jbuf[0, h] += ee_r * qr + ee_i * qi
                jbuf[1, h] += eo_i * qr - eo_r * qi
                jbuf[2, h] += oe_i * qr - oe_r * qi
                jbuf[3, h] += oo_r * qr + oo_i * qi
        return carry

    lax.fori_loop(0, CONDS, backward, 0)

    for h in range(2):
        sign_u = 1.0 - 2.0 * h
        aown[h * UH : (h + 1) * UH, :] = (
            jbuf[0, h]
            + swap(sign_v * jbuf[1, h])
            - sign_u * jbuf[2, 1 - h]
            + swap(sign_u * sign_v * jbuf[3, 1 - h])
        )

    def adjoint_part(mask):
        return remote(aown, ain.at[mask - 1], as_sem.at[mask - 1], ar_sem.at[mask - 1], partner(mask))

    def adjoint_prev():
        return remote(aown, anear.at[c], as_sem.at[3], near_sem.at[c], (t - 1, GROUP - 1))

    def adjoint_next():
        return remote(aown, anear.at[c], as_sem.at[4], near_sem.at[c], (t + 1, 0))

    def adjoint_near(other):
        return remote(aown, anear.at[other], as_sem.at[3], near_sem.at[other], (t, c ^ 1))

    @pl.when(has_prev)
    def _():
        adjoint_prev().start()

    @pl.when(has_next)
    def _():
        adjoint_next().start()

    for mask in range(1, GROUP):
        adjoint_part(mask).start()

    near = (first & has_prev) | (final & has_next)

    @pl.when(jnp.logical_not(near))
    def _():
        anear[...] = jnp.zeros_like(anear)

    factor = grad_v
    factor[...] = (MASK_STEEP / (SIZE * SIZE)) * (1.0 - jnp.square(jnp.tanh(MASK_STEEP * theta_v[...])))

    for mask in range(1, GROUP):
        adjoint_part(mask).wait_recv()

    @pl.when(near)
    def _():
        for other in range(GROUP):
            adjoint_near(other).wait_recv()

    rows = []
    for value in (aown[...] + ain[0] + ain[1] + ain[2], anear[0] + anear[1] + anear[2] + anear[3]):
        hi, lo = split(value)
        rows += [hi, hi, lo, jnp.zeros((256 - 3 * UR, VR), BF)]
    tall = dot(pack[...], jnp.concatenate(rows, axis=0))
    hi, lo = split(tall)
    grad_v[...] = dot(jnp.concatenate([hi, lo, hi], axis=1), bt[...]) * factor[...]
    out = pltpu.make_async_copy(grad_v, out_h, out_sem)
    out.start()

    @pl.when(has_next & final)
    def _():
        for other in range(GROUP):
            halo_next(other).wait_send()

    @pl.when(has_prev & first)
    def _():
        for other in range(GROUP):
            halo_prev(other).wait_send()

    for mask in range(1, GROUP):
        part(mask).wait_send()
        kernels_to(mask).wait_send()
        adjoint_part(mask).wait_send()

    @pl.when(has_prev)
    def _():
        adjoint_prev().wait_send()

    @pl.when(has_next)
    def _():
        adjoint_next().wait_send()

    out.wait()


def shards(tiles, theta, target, kernel_real, kernel_imag, weights, thresholds):
    constants = tables()
    anywhere = pl.BlockSpec(memory_space=pl.ANY)
    scalars = pl.BlockSpec(memory_space=pltpu.SMEM)
    dma = pltpu.SemaphoreType.DMA
    local = (LOCAL, KERNELS)
    by, bt, pack, turned, pv, pu = constants
    call = pl.pallas_call(
        functools.partial(kernel, tiles),
        out_shape=jax.ShapeDtypeStruct((ROWS, TP), F32),
        in_specs=[anywhere] * 4 + [scalars] * 2 + [anywhere] * 6,
        out_specs=anywhere,
        scratch_shapes=[
            pltpu.VMEM((ROWS, TP), F32),
            pltpu.VMEM((ROWS, TP), jnp.int32),
            pltpu.VMEM((2,) + local + (KSUP, KSUP), F32),
            pltpu.VMEM(by.shape, BF),
            pltpu.VMEM(bt.shape, BF),
            pltpu.VMEM(pack.shape[1:], BF),
            pltpu.VMEM(turned.shape[1:], BF),
            pltpu.VMEM(pv.shape, BF),
            pltpu.VMEM(pu.shape, BF),
            pltpu.VMEM((LOCAL * KERNELS * 2 * UR, VR), F32),
            pltpu.VMEM((GROUP,) + local + (2, UR, VR), F32),
            pltpu.VMEM((UR, VR), F32),
            pltpu.VMEM((UR, VR), F32),
            pltpu.VMEM((5, UR, VR), F32),
            pltpu.VMEM((4, 2, UH, VR), F32),
            pltpu.VMEM((UR, VR), F32),
            pltpu.VMEM((3, UR, VR), F32),
            pltpu.VMEM((GROUP, UR, VR), F32),
            pltpu.VMEM((4, 2, UH, VR), F32),
            pltpu.VMEM((CONDS, KERNELS, 2 * ROWS, TP), F32),
            pltpu.VMEM((CONDS, ROWS, TP), F32),
            pltpu.VMEM((ROWS, TP), F32),
            pltpu.VMEM((ROWS, TP), F32),
            dma((10,)),
            dma((3,)),
            dma((3,)),
            dma((3,)),
            dma((3,)),
            dma((4,)),
            dma((2,)),
            dma((5,)),
            dma((3,)),
            dma((4,)),
            dma,
        ],
        compiler_params=pltpu.CompilerParams(collective_id=0, has_side_effects=True),
        name="window_gradient",
    )
    return call(theta, target, kernel_real, kernel_imag, weights, thresholds, *(jnp.asarray(x) for x in constants))


def solution(mesh):
    in_specs = (
        P(("tile", "cond"), None),
        P("tile", None),
        P("cond", None, None, None),
        P("cond", None, None, None),
        P(),
        P("cond"),
    )
    out_specs = P(("tile", "cond"), None)
    body = functools.partial(shards, mesh.shape["tile"])
    return jax.shard_map(body, mesh=mesh, in_specs=in_specs, out_specs=out_specs, check_vma=False)
```

profile of v0, /device:TPU:6, one launch (start us, length us, event | category | flops | bytes accessed | tf_op | source)
XLA Modules:
  0.0 51.3 jit_solution(5680458939315149738)
XLA Ops:
  0.0 0.0 copy-start
  0.0 1.6 %copy.13.kr_h = f32[2,2,65,65]{3,2,1,0:T(8,128)} copy(f32[2,2,65,65]{3,1,2,0:T(2,128)} %param.14) | data formatting | bytes 135200 | tf_op args[2]
  1.6 0.0 copy-done
  1.6 0.7 %copy.14.ki_h = f32[2,2,65,65]{3,2,1,0:T(8,128)} copy(f32[2,2,65,65]{3,1,2,0:T(2,128)S(1)} %copy-done) | data formatting | bytes 135200 | tf_op args[3]
  2.3 47.3 %window_gradient.1 = f32[128,512]{1,0:T(8,128)} custom-call(f32[128,512]{1,0:T(8,128)} %theta_h.1, s32[512,512]{1,0:T(8,128)} %target_h.1, f32[2,2,65,65]{3,2,1,0:T(8,128)} %copy.13.kr_h, f32[2,2,65,65]{3,2,1,0:T(8,128)} %copy.14.ki_h, s32[8]{0:T(128)} %weights_s.1, f32[2]{0:T(128)} %thresholds_s.1, bf16[512,256]{1,0:T(8,128)(2,1)} %constant.12.clone.by_h, ...), custom_call_target="tpu_custom_call" | custom-call | tf_op jit(solution)/shard_map/window_gradient/pallas_call | solution.py:491
  49.6 1.7 %copy.16 = f32[128,512]{1,0:T(8,128)} copy(f32[128,512]{1,0:T(8,128)} %window_gradient.1) | data formatting | bytes 524288
Async XLA Ops:
  0.0 1.6 %copy-start = (f32[2,2,65,65]{3,1,2,0:T(2,128)S(1)}, f32[2,2,65,65]{3,1,2,0:T(2,128)}, u32[]{:S(2)}) copy-start(f32[2,2,65,65]{3,1,2,0:T(2,128)} %param.15) | copy-start | bytes 202804
where the time goes:
time: 51.5 us; the launch traced here: 51.3 us
  Pallas kernels  47.3 us (92%)
  local copies, waits for them, and re-layouts  3.96 us (8%)
    pallas_call x1, Pallas kernels, shards(): call(theta, target, kernel_real, kernel_imag, weights, thresholds, *(jnp....  47.3 us
    unnamed x5, local copies, waits for them, and re-layouts  3.96 us

commit v1 on v0

--- a/solution.py
+++ b/solution.py
@@ -105,7 +105,7 @@
     theta_h, target_h, kr_h, ki_h, weights_s, thresholds_s, by_h, bt_h, pack_h, turned_h, pv_h, pu_h,
     out_h,
     theta_v, target_v, raw_v, by, bt, pack, turned, pv, pu,
-    stack, zbuf, rown, rhalo, rin, rsum, aown, ain, anear, jbuf, amps, resists, band, grad_v,
+    stack, zbuf, rown, rhalo, rin, rsum, aown, ain, anear, jbuf, amps, resists, band, wanted, grad_v,
     load_sem, zs_sem, zr_sem, rs_sem, rr_sem, hs_sem, hr_sem, as_sem, ar_sem, near_sem, out_sem,
 ):
     t = lax.axis_index("tile")
@@ -142,8 +142,10 @@
     def greet(device):
         pl.semaphore_signal(barrier, inc=1, device_id=device, device_id_type=MESH)
 
+    mirror = ((t + tiles // 2) % tiles, c ^ 2)
     for mask in range(1, GROUP):
         greet(partner(mask))
+    greet(mirror)
     for other in range(GROUP):
         @pl.when(has_next & (final | (other == 0)))
         def _(other=other):
@@ -160,7 +162,7 @@
         for l in range(LOCAL):
             for k in range(KERNELS):
                 at = ((l * KERNELS + k) * 2 + ri) * UR
-                stack[at : at + KSUP, 0:KSUP] = raw_v[ri, l, k]
+                stack[at : at + KSUP, 0:KSUP] = raw_v[ri, l, :, k, :]
     load_pv.wait()
     load_pu.wait()
     hi, lo = split(stack[...])
@@ -186,7 +188,7 @@
 
     across_next = jnp.where(final, GROUP, 1) * has_next.astype(jnp.int32)
     across_prev = jnp.where(first, GROUP, 1) * has_prev.astype(jnp.int32)
-    pl.semaphore_wait(barrier, GROUP - 1 + across_next + across_prev)
+    pl.semaphore_wait(barrier, GROUP + across_next + across_prev)
 
     def remote(src, dst, send, recv, device):
         return pltpu.make_async_remote_copy(
@@ -203,7 +205,9 @@
         return remote(rown, rin.at[mask - 1], rs_sem.at[mask - 1], rr_sem.at[mask - 1], partner(mask))
 
     def kernels_to(mask):
-        return remote(zbuf.at[0], zbuf.at[mask], zs_sem.at[mask - 1], zr_sem.at[mask - 1], partner(mask))
+        device = partner(1) if mask != 2 else mirror
+        source = 2 if mask == 3 else 0
+        return remote(zbuf.at[source], zbuf.at[mask], zs_sem.at[mask - 1], zr_sem.at[mask - 1], device)
 
     @pl.when(has_next & final)
     def _():
@@ -217,7 +221,7 @@
 
     for mask in range(1, GROUP):
         part(mask).start()
-    for mask in range(1, GROUP):
+    for mask in (2, 1):
         kernels_to(mask).start()
 
     @pl.when(jnp.logical_not(has_prev))
@@ -270,16 +274,24 @@
     load_pack.wait()
     load_bt.wait()
 
-    def forward(i, carry):
-        s = i // LOCAL
-        l = i % LOCAL
-
-        @pl.when((l == 0) & (s > 0))
+    each = [(l, k) for l in range(LOCAL) for k in range(KERNELS)]
+
+    def forward(s, carry):
+        @pl.when(s == 1)
         def _():
-            remote(zbuf.at[0], zbuf.at[s], zs_sem.at[s - 1], zr_sem.at[s - 1], (t, c ^ 1)).wait_recv()
-
-        intensity = None
-        for k in range(KERNELS):
+            kernels_to(1).wait_recv()
+
+        @pl.when(s == 2)
+        def _():
+            kernels_to(2).wait_recv()
+            kernels_to(3).start()
+
+        @pl.when(s == 3)
+        def _():
+            kernels_to(3).wait_recv()
+
+        grids = []
+        for l, k in each:
             ee_r, eo_r, oe_r, oo_r, ee_i, eo_i, oe_i, oo_i = parts_of(s, l, k)
             real = []
             imag = []
@@ -287,32 +299,39 @@
                 r0, r1, r2, r3 = (rsum[n, h] for n in range(4))
                 real.append(ee_r * r0 + eo_i * r1 + oe_i * r2 + oo_r * r3)
                 imag.append(ee_i * r0 - eo_r * r1 - oe_r * r2 + oo_i * r3)
-            grid = jnp.concatenate(
-                [jnp.concatenate(real, axis=0), jnp.concatenate(imag, axis=0)], axis=1
-            )
+            grid = jnp.concatenate([jnp.concatenate(real, axis=0), jnp.concatenate(imag, axis=0)], axis=1)
             hi, lo = split(grid)
-            tall = dot(pack[:, : 3 * UR], jnp.concatenate([hi, hi, lo], axis=0))
+            grids.append(jnp.concatenate([hi, hi, lo], axis=0))
+        lhs = []
+        for grid in grids:
+            tall = dot(pack[:, : 3 * UR], grid)
             tall = jnp.concatenate([tall[:, :VR], tall[:, VR:]], axis=0)
             hi, lo = split(tall)
-            amp = dot(jnp.concatenate([hi, lo, hi], axis=1), bt[...])
-            amps[i, k] = amp
-            power = amp[:ROWS] * amp[:ROWS] + amp[ROWS:] * amp[ROWS:]
-            intensity = power if intensity is None else intensity + power
-        level = zbuf[s, l, 0, 0, HALF + 2 : HALF + 3, 0:1]
-        resist = jax.nn.sigmoid(RESIST_STEEP * (intensity - level))
-        resists[i] = resist
-
-        @pl.when(i == 0)
+            lhs.append(jnp.concatenate([hi, lo, hi], axis=1))
+        amp = dot(jnp.concatenate(lhs, axis=0), bt[...])
+        amps[s] = amp
+        total = None
+        for l in range(LOCAL):
+            intensity = None
+            for part in range(4):
+                piece = amp[(l * 4 + part) * ROWS : (l * 4 + part + 1) * ROWS]
+                intensity = piece * piece if part == 0 else intensity + piece * piece
+            level = zbuf[s, l, 0, 0, HALF + 2 : HALF + 3, 0:1]
+            resist = jax.nn.sigmoid(RESIST_STEEP * (intensity - level))
+            resists[s, l] = resist
+            total = resist if l == 0 else total + resist
+
+        @pl.when(s == 0)
         def _():
-            band[...] = resist
-
-        @pl.when(i > 0)
+            band[...] = total
+
+        @pl.when(s > 0)
         def _():
-            band[...] += resist
+            band[...] += total
 
         return carry
 
-    lax.fori_loop(0, CONDS, forward, 0)
+    lax.fori_loop(0, GROUP, forward, 0)
 
     load_target.wait()
     weight_sum = weights_s[0]
@@ -320,37 +339,48 @@
         weight_sum = weight_sum + weights_s[n]
     weight_sum = jnp.full((8, TP), weight_sum, jnp.int32).astype(F32)
     jbuf[...] = jnp.zeros_like(jbuf)
-
-    def backward(i, carry):
-        s = i // LOCAL
-        l = i % LOCAL
-        weight = jnp.full((8, TP), weights_s[(c ^ s) * LOCAL + l], jnp.int32).astype(F32) / weight_sum
-        weight = weight[0:1]
-        resist = resists[i]
-        slope = 2.0 * weight * (resist - target_v[...].astype(F32)) + (2.0 * BAND_WEIGHT / CONDS) * (
-            resist - band[...] * (1.0 / CONDS)
-        )
-        field = 2.0 * slope * RESIST_STEEP * resist * (1.0 - resist)
-        field = jnp.concatenate([field, field], axis=0)
-        for k in range(KERNELS):
-            hi, lo = split(field * amps[i, k])
-            wide = dot(jnp.concatenate([hi, lo], axis=0), by[...])
-            drive = wide[: 2 * ROWS, :VR] + wide[: 2 * ROWS, VR:] + wide[2 * ROWS :, :VR]
-            drive = jnp.concatenate([drive[:ROWS], drive[ROWS:]], axis=1)
-            hi, lo = split(drive)
+    wanted[...] = target_v[...].astype(F32)
+    band[...] = band[...] * (4.0 * RESIST_STEEP * BAND_WEIGHT / CONDS / CONDS)
+
+    def backward(s, carry):
+        drives = []
+        for l in range(LOCAL):
+            weight = jnp.full((8, TP), weights_s[(c ^ s) * LOCAL + l], jnp.int32).astype(F32) / weight_sum
+            pull = (4.0 * RESIST_STEEP) * weight[0:1]
+            resist = resists[s, l]
+            slope = (pull + 4.0 * RESIST_STEEP * BAND_WEIGHT / CONDS) * resist - (pull * wanted[...] + band[...])
+            field = slope * (resist - resist * resist)
+            for part in range(4):
+                at = (l * 4 + part) * ROWS
+                drives.append(field * amps[s, at : at + ROWS])
+        hi, lo = split(jnp.concatenate(drives, axis=0))
+        wide = dot(jnp.concatenate([hi, lo], axis=0), by[...])
+        half = 8 * ROWS
+        drive = wide[:half, :VR] + wide[:half, VR:] + wide[half:, :VR]
+        sums = [[None, None] for _ in range(4)]
+        for n, (l, k) in enumerate(each):
+            pair = jnp.concatenate([drive[2 * n * ROWS : (2 * n + 1) * ROWS], drive[(2 * n + 1) * ROWS : (2 * n + 2) * ROWS]], axis=1)
+            hi, lo = split(pair)
             back = dot(turned[: 2 * UR, :], jnp.concatenate([hi, lo], axis=0))
             back = back[:UR] + back[UR:]
             ee_r, eo_r, oe_r, oo_r, ee_i, eo_i, oe_i, oo_i = parts_of(s, l, k)
             for h in range(2):
                 qr = back[h * UH : (h + 1) * UH, :VR]
                 qi = back[h * UH : (h + 1) * UH, VR:]
-                jbuf[0, h] += ee_r * qr + ee_i * qi
-                jbuf[1, h] += eo_i * qr - eo_r * qi
-                jbuf[2, h] += oe_i * qr - oe_r * qi
-                jbuf[3, h] += oo_r * qr + oo_i * qi
+                terms = (
+                    ee_r * qr + ee_i * qi,
+                    eo_i * qr - eo_r * qi,
+                    oe_i * qr - oe_r * qi,
+                    oo_r * qr + oo_i * qi,
+                )
+                for m, term in enumerate(terms):
+                    sums[m][h] = term if n == 0 else sums[m][h] + term
+        for m in range(4):
+            for h in range(2):
+                jbuf[m, h] += sums[m][h]
         return carry
 
-    lax.fori_loop(0, CONDS, backward, 0)
+    lax.fori_loop(0, GROUP, backward, 0)
 
     for h in range(2):
         sign_u = 1.0 - 2.0 * h
@@ -452,7 +482,7 @@
         scratch_shapes=[
             pltpu.VMEM((ROWS, TP), F32),
             pltpu.VMEM((ROWS, TP), jnp.int32),
-            pltpu.VMEM((2,) + local + (KSUP, KSUP), F32),
+            pltpu.VMEM((2, LOCAL, KSUP, KERNELS, KSUP), F32),
             pltpu.VMEM(by.shape, BF),
             pltpu.VMEM(bt.shape, BF),
             pltpu.VMEM(pack.shape[1:], BF),
@@ -469,8 +499,9 @@
             pltpu.VMEM((3, UR, VR), F32),
             pltpu.VMEM((GROUP, UR, VR), F32),
             pltpu.VMEM((4, 2, UH, VR), F32),
-            pltpu.VMEM((CONDS, KERNELS, 2 * ROWS, TP), F32),
-            pltpu.VMEM((CONDS, ROWS, TP), F32),
+            pltpu.VMEM((GROUP, LOCAL * KERNELS * 2 * ROWS, TP), F32),
+            pltpu.VMEM((GROUP, LOCAL, ROWS, TP), F32),
+            pltpu.VMEM((ROWS, TP), F32),
             pltpu.VMEM((ROWS, TP), F32),
             pltpu.VMEM((ROWS, TP), F32),
             dma((10,)),
@@ -488,6 +519,7 @@
         compiler_params=pltpu.CompilerParams(collective_id=0, has_side_effects=True),
         name="window_gradient",
     )
+    kernel_real, kernel_imag = (jnp.swapaxes(x, 1, 2) for x in (kernel_real, kernel_imag))
     return call(theta, target, kernel_real, kernel_imag, weights, thresholds, *(jnp.asarray(x) for x in constants))
 
 

time: 51.5 us -> 34.9 us (0.68)
  the two profiles are of different devices: /device:TPU:6 before, /device:TPU:2 now
where the time goes in v1:
time: 34.9 us; the launch traced here: 34.5 us
  Pallas kernels  32.8 us (94%)
  local copies, waits for them, and re-layouts  1.67 us (5%)
    pallas_call x1, Pallas kernels, shards(): call(theta, target, kernel_real, kernel_imag, weights, thresholds, *(jnp....  32.8 us
    unnamed x1, local copies, waits for them, and re-layouts  1.67 us

profile of v1, /device:TPU:2, one launch (start us, length us, event | category | flops | bytes accessed | tf_op | source)
XLA Modules:
  0.0 34.5 jit_solution(8531464942366275686)
XLA Ops:
  0.0 32.8 %window_gradient.1 = f32[128,512]{1,0:T(8,128)} custom-call(f32[128,512]{1,0:T(8,128)} %theta_h.1, s32[512,512]{1,0:T(8,128)} %target_h.1, f32[2,65,2,65]{3,2,1,0:T(2,128)} %bitcast.2, f32[2,65,2,65]{3,2,1,0:T(2,128)} %bitcast.3, s32[8]{0:T(128)} %weights_s.1, f32[2]{0:T(128)} %thresholds_s.1, bf16[512,256]{1,0:T(8,128)(2,1)} %constant.12.clone.by_h, ...), custom_call_target="tpu_custom_call" | custom-call | tf_op jit(solution)/shard_map/window_gradient/pallas_call | solution.py:523
  32.8 1.7 %copy.14 = f32[128,512]{1,0:T(8,128)} copy(f32[128,512]{1,0:T(8,128)} %window_gradient.1) | data formatting | bytes 524288

commit v2 on v1

--- a/solution.py
+++ b/solution.py
@@ -22,8 +22,11 @@
 LOCAL = CONDS // GROUP
 UH = 40
 UR = 2 * UH
-VH = 64
-VR = 2 * VH
+VR = 128
+FLAT = 2 * HALF
+DEPTH = LOCAL * KERNELS
+EDGE = DEPTH * UR
+SPARE = HALF + 1
 
 MASK_STEEP = 2.0
 RESIST_STEEP = 4.0
@@ -44,42 +47,65 @@
     return hi, (x - hi.astype(np.float64)).astype(ml_dtypes.bfloat16)
 
 
-def basis(positions, pitch):
+def waves(positions):
     phase = (np.asarray(positions)[:, None] * np.arange(HALF + 1)[None, :]) % SIZE
     angles = phase * (2.0 * math.pi / SIZE)
-    out = np.zeros((len(positions), 2 * pitch))
-    out[:, : HALF + 1] = np.cos(angles)
-    out[:, pitch : pitch + HALF + 1] = np.sin(angles)
-    out[:, pitch] = 0.0
+    return np.cos(angles), np.sin(angles)
+
+
+def row_basis(positions):
+    cos, sin = waves(positions)
+    out = np.zeros((len(positions), UR))
+    out[:, : HALF + 1] = cos
+    out[:, UH + 1 : UH + HALF + 1] = sin[:, 1:]
     return out
 
 
-def parity(pitch, columns):
-    out = np.zeros((2 * pitch, columns))
+def column_basis(positions):
+    cos, sin = waves(positions)
+    out = np.zeros((len(positions), VR))
+    out[:, :HALF] = cos[:, 1:]
+    out[:, HALF:FLAT] = sin[:, 1:]
+    out[:, FLAT] = 1.0
+    return out
+
+
+def parity_rows():
+    out = np.zeros((UR, UR))
     out[0, HALF] = 1.0
     for j in range(1, HALF + 1):
-        out[j, HALF + j] = 1.0
-        out[j, HALF - j] = 1.0
-        out[pitch + j, HALF + j] = 1.0
-        out[pitch + j, HALF - j] = -1.0
+        out[j, HALF + j] = out[j, HALF - j] = out[UH + j, HALF + j] = 1.0
+        out[UH + j, HALF - j] = -1.0
+    return out
+
+
+def parity_columns():
+    out = np.zeros((2 * VR, 2 * VR))
+    for ri in range(2):
+        out[ri * VR + HALF, VR + ri] = 1.0
+        for j in range(1, HALF + 1):
+            even = ri * FLAT + j - 1
+            out[ri * VR + HALF + j, even] = out[ri * VR + HALF - j, even] = 1.0
+            out[ri * VR + HALF + j, even + HALF] = 1.0
+            out[ri * VR + HALF - j, even + HALF] = -1.0
     return out
 
 
 def tables():
     bf = ml_dtypes.bfloat16
-    cols = basis(np.arange(TP) + HALO, VH)
+    cols = column_basis(np.arange(TP) + HALO)
     hi, lo = np_split(cols)
     by = np.concatenate([hi, lo], axis=1)
     bt = np.concatenate([hi.T, hi.T, lo.T], axis=0)
     pack = []
     turned = []
     for c in range(GROUP):
-        own = basis(np.arange(ROWS) + HALO + ROWS * c, UH)
+        own = row_basis(np.arange(ROWS) + HALO + ROWS * c)
         near = np.zeros_like(own)
         if c == 0:
-            near[:HALO] = basis(np.arange(HALO) + HALO + TP, UH)
+            near[:HALO] = row_basis(np.arange(HALO) + HALO + TP)
         if c == GROUP - 1:
-            near[ROWS - HALO :] = basis(np.arange(HALO), UH)
+            near[ROWS - HALO :] = row_basis(np.arange(HALO))
         row = []
         column = []
         for table in (own, near):
@@ -89,9 +115,9 @@
             column.append(np.concatenate([tlo.T, np.zeros((UR, ROWS), bf)], axis=1))
         pack.append(np.concatenate(row, axis=1))
         turned.append(np.concatenate(column, axis=0))
-    pv = parity(VH, VR).T.astype(bf)
+    pv = parity_columns().astype(bf)
     pv = np.concatenate([pv, pv], axis=0)
-    pu = parity(UH, UR).astype(bf)
+    pu = parity_rows().astype(bf)
     pu = np.concatenate([pu, pu], axis=1)
     return by, bt, np.stack(pack), np.stack(turned), pv, pu
 
@@ -105,7 +131,7 @@
     theta_h, target_h, kr_h, ki_h, weights_s, thresholds_s, by_h, bt_h, pack_h, turned_h, pv_h, pu_h,
     out_h,
     theta_v, target_v, raw_v, by, bt, pack, turned, pv, pu,
-    stack, zbuf, rown, rhalo, rin, rsum, aown, ain, anear, jbuf, amps, resists, band, wanted, grad_v,
+    stack, zbuf, coef, rown, rhalo, rin, rsum, aown, ain, anear, jbuf, amps, resists, band, wanted, grad_v,
     load_sem, zs_sem, zr_sem, rs_sem, rr_sem, hs_sem, hr_sem, as_sem, ar_sem, near_sem, out_sem,
 ):
     t = lax.axis_index("tile")
@@ -155,24 +181,65 @@
         def _(other=other):
             greet((t - 1, other))
 
+    lane = lax.broadcasted_iota(jnp.int32, (UH, VR), 1)
+    row = lax.broadcasted_iota(jnp.int32, (UH, VR), 0)
+    tall_lane = lax.broadcasted_iota(jnp.int32, (UR, VR), 1)
+    diagonal = tall_lane == lax.broadcasted_iota(jnp.int32, (UR, VR), 0)
+    sign_v = jnp.where((lane >= HALF) & (lane < FLAT), -1.0, 1.0).astype(F32)
+
+    def swap(x):
+        out = jnp.where(lane < HALF, pltpu.roll(x, VR - HALF, 1), pltpu.roll(x, HALF, 1))
+        return jnp.where(lane < FLAT, out, 0.0)
+
+    def packed(x):
+        out = jnp.where(lane < FLAT, x[:UH], pltpu.roll(x[UH:], FLAT, 1))
+        flat = jnp.sum(jnp.where(diagonal, x[:, FLAT : FLAT + 1], 0.0), axis=0, keepdims=True)
+        return jnp.where(row == SPARE, flat, out)
+
+    def unpacked(x):
+        flat = jnp.sum(jnp.where(diagonal, x[SPARE : SPARE + 1], 0.0), axis=1, keepdims=True)
+        keep = (lane < FLAT) & (row < SPARE)
+        out = []
+        for h, value in enumerate((x, pltpu.roll(x, FLAT, 1))):
+            out.append(jnp.where(lane == FLAT, flat[h * UH : (h + 1) * UH], jnp.where(keep, value, 0.0)))
+        return out
+
+    def unpack_kernels(s):
+        edge = zbuf[s, EDGE:, :]
+        for n in range(DEPTH):
+            p = zbuf[s, n * UR : (n + 1) * UR, :]
+            p32, p64, p96 = (pltpu.roll(p, shift, 1) for shift in (HALF, 2 * HALF, 3 * HALF))
+            first_half = tall_lane < HALF
+            for at, (a, b) in enumerate(((p, p32), (p96, p), (p64, p96), (p32, p64))):
+                value = jnp.where(first_half, a, b)
+                if at % 2 == 0:
+                    flat = pltpu.roll(edge, FLAT - (2 * n + at // 2), 1)
+                    value = jnp.where(tall_lane == FLAT, flat, value)
+                coef[s, n, at] = value
+
     stack[...] = jnp.zeros_like(stack)
     load_kr.wait()
     load_ki.wait()
     for ri in range(2):
         for l in range(LOCAL):
             for k in range(KERNELS):
-                at = ((l * KERNELS + k) * 2 + ri) * UR
-                stack[at : at + KSUP, 0:KSUP] = raw_v[ri, l, :, k, :]
+                at = (l * KERNELS + k) * UR
+                stack[at : at + KSUP, ri * VR : ri * VR + KSUP] = raw_v[ri, l, :, k, :]
     load_pv.wait()
     load_pu.wait()
     hi, lo = split(stack[...])
     folded = dot(jnp.concatenate([hi, lo], axis=1), pv[...])
     hi, lo = split(folded)
-    for n in range(LOCAL * KERNELS * 2):
+    edge = None
+    for n in range(DEPTH):
         rhs = jnp.concatenate([hi[n * UR : (n + 1) * UR], lo[n * UR : (n + 1) * UR]], axis=0)
-        zbuf[0, n // 4, (n // 2) % 2, n % 2] = dot(pu[...], rhs)
+        value = dot(pu[...], rhs)
+        zbuf[0, n * UR : (n + 1) * UR, :] = value[:, :VR]
+        value = value[:, VR:]
+        edge = value if n == 0 else edge + pltpu.roll(value, 2 * n, 1)
+    zbuf[0, EDGE:, :] = edge
     for l in range(LOCAL):
-        zbuf[0, l, 0, 0, HALF + 2 : HALF + 3, :] = jnp.full((1, VR), thresholds_s[l], F32)
+        zbuf[0, EDGE + SPARE + l : EDGE + SPARE + l + 1, :] = jnp.full((1, VR), thresholds_s[l], F32)
 
     load_theta.wait()
     load_by.wait()
@@ -183,8 +250,8 @@
     column = wide[:ROWS, :VR] + wide[:ROWS, VR:] + wide[ROWS:, :VR]
     hi, lo = split(column)
     both = dot(turned[...], jnp.concatenate([hi, lo], axis=0))
-    rown[...] = both[:UR] + both[UR : 2 * UR]
-    rhalo[...] = both[2 * UR : 3 * UR] + both[3 * UR :]
+    rown[...] = packed(both[:UR] + both[UR : 2 * UR])
+    rhalo[...] = packed(both[2 * UR : 3 * UR] + both[3 * UR :])
 
     across_next = jnp.where(final, GROUP, 1) * has_next.astype(jnp.int32)
     across_prev = jnp.where(first, GROUP, 1) * has_prev.astype(jnp.int32)
@@ -226,11 +293,15 @@
 
     @pl.when(jnp.logical_not(has_prev))
     def _():
-        rin[3] = jnp.zeros((UR, VR), F32)
+        rin[3] = jnp.zeros((UH, VR), F32)
 
     @pl.when(jnp.logical_not(has_next))
     def _():
-        rin[4] = jnp.zeros((UR, VR), F32)
+        rin[4] = jnp.zeros((UH, VR), F32)
+
+    unpack_kernels(0)
+    kernels_to(1).wait_recv()
+    unpack_kernels(1)
 
     @pl.when(has_prev)
     def _():
@@ -243,60 +314,40 @@
     for mask in range(1, GROUP):
         part(mask).wait_recv()
 
-    lane = lax.broadcasted_iota(jnp.int32, (UH, VR), 1)
-    low = lane < VH
-    sign_v = jnp.where(low, 1.0, -1.0).astype(F32)
-
-    def swap(x):
-        return pltpu.roll(x, VH, 1)
-
     total = rown[...] + rin[0] + rin[1] + rin[2] + rin[3] + rin[4]
-    total = total * (1.0 / (SIZE * SIZE))
+    halves = unpacked(total * (1.0 / (SIZE * SIZE)))
     for h in range(2):
-        here = total[h * UH : (h + 1) * UH]
-        there = total[(1 - h) * UH : (2 - h) * UH]
         sign_u = 1.0 - 2.0 * h
-        rsum[0, h] = here
-        rsum[1, h] = sign_v * swap(here)
-        rsum[2, h] = sign_u * there
-        rsum[3, h] = (-sign_u) * sign_v * swap(there)
-
-    def parts_of(s, l, k):
-        out = []
-        for ri in range(2):
-            for h in range(2):
-                z = zbuf[s, l, k, ri, h * UH : (h + 1) * UH, :]
-                turn = swap(z)
-                out.append(jnp.where(low, z, turn))
-                out.append(jnp.where(low, turn, z))
-        return out
+        rsum[0, h] = halves[h]
+        rsum[1, h] = sign_v * swap(halves[h])
+        rsum[2, h] = sign_u * halves[1 - h]
+        rsum[3, h] = (-sign_u) * sign_v * swap(halves[1 - h])
+
+    def parts_of(s, n):
+        return [coef[s, n, 2 * ri + v, u * UH : (u + 1) * UH, :] for ri in range(2) for u in range(2) for v in range(2)]
 
     load_pack.wait()
     load_bt.wait()
 
-    each = [(l, k) for l in range(LOCAL) for k in range(KERNELS)]
-
     def forward(s, carry):
-        @pl.when(s == 1)
-        def _():
-            kernels_to(1).wait_recv()
-
         @pl.when(s == 2)
         def _():
             kernels_to(2).wait_recv()
             kernels_to(3).start()
+            unpack_kernels(2)
 
         @pl.when(s == 3)
         def _():
             kernels_to(3).wait_recv()
+            unpack_kernels(3)
 
         grids = []
-        for l, k in each:
-            ee_r, eo_r, oe_r, oo_r, ee_i, eo_i, oe_i, oo_i = parts_of(s, l, k)
+        for n in range(DEPTH):
+            ee_r, eo_r, oe_r, oo_r, ee_i, eo_i, oe_i, oo_i = parts_of(s, n)
             real = []
             imag = []
             for h in range(2):
-                r0, r1, r2, r3 = (rsum[n, h] for n in range(4))
+                r0, r1, r2, r3 = (rsum[m, h] for m in range(4))
                 real.append(ee_r * r0 + eo_i * r1 + oe_i * r2 + oo_r * r3)
                 imag.append(ee_i * r0 - eo_r * r1 - oe_r * r2 + oo_i * r3)
             grid = jnp.concatenate([jnp.concatenate(real, axis=0), jnp.concatenate(imag, axis=0)], axis=1)
@@ -316,7 +367,7 @@
             for part in range(4):
                 piece = amp[(l * 4 + part) * ROWS : (l * 4 + part + 1) * ROWS]
                 intensity = piece * piece if part == 0 else intensity + piece * piece
-            level = zbuf[s, l, 0, 0, HALF + 2 : HALF + 3, 0:1]
+            level = zbuf[s, EDGE + SPARE + l : EDGE + SPARE + l + 1, 0:1]
             resist = jax.nn.sigmoid(RESIST_STEEP * (intensity - level))
             resists[s, l] = resist
             total = resist if l == 0 else total + resist
@@ -358,12 +409,12 @@
         half = 8 * ROWS
         drive = wide[:half, :VR] + wide[:half, VR:] + wide[half:, :VR]
         sums = [[None, None] for _ in range(4)]
-        for n, (l, k) in enumerate(each):
+        for n in range(DEPTH):
             pair = jnp.concatenate([drive[2 * n * ROWS : (2 * n + 1) * ROWS], drive[(2 * n + 1) * ROWS : (2 * n + 2) * ROWS]], axis=1)
             hi, lo = split(pair)
             back = dot(turned[: 2 * UR, :], jnp.concatenate([hi, lo], axis=0))
             back = back[:UR] + back[UR:]
-            ee_r, eo_r, oe_r, oo_r, ee_i, eo_i, oe_i, oo_i = parts_of(s, l, k)
+            ee_r, eo_r, oe_r, oo_r, ee_i, eo_i, oe_i, oo_i = parts_of(s, n)
             for h in range(2):
                 qr = back[h * UH : (h + 1) * UH, :VR]
                 qi = back[h * UH : (h + 1) * UH, VR:]
@@ -382,14 +433,16 @@
 
     lax.fori_loop(0, GROUP, backward, 0)
 
+    halves = []
     for h in range(2):
         sign_u = 1.0 - 2.0 * h
-        aown[h * UH : (h + 1) * UH, :] = (
+        halves.append(
             jbuf[0, h]
             + swap(sign_v * jbuf[1, h])
             - sign_u * jbuf[2, 1 - h]
             + swap(sign_u * sign_v * jbuf[3, 1 - h])
         )
+    aown[...] = packed(jnp.concatenate(halves, axis=0))
 
     def adjoint_part(mask):
         return remote(aown, ain.at[mask - 1], as_sem.at[mask - 1], ar_sem.at[mask - 1], partner(mask))
@@ -433,7 +486,7 @@
 
     rows = []
     for value in (aown[...] + ain[0] + ain[1] + ain[2], anear[0] + anear[1] + anear[2] + anear[3]):
-        hi, lo = split(value)
+        hi, lo = split(jnp.concatenate(unpacked(value), axis=0))
         rows += [hi, hi, lo, jnp.zeros((256 - 3 * UR, VR), BF)]
     tall = dot(pack[...], jnp.concatenate(rows, axis=0))
     hi, lo = split(tall)
@@ -472,7 +525,6 @@
     anywhere = pl.BlockSpec(memory_space=pl.ANY)
     scalars = pl.BlockSpec(memory_space=pltpu.SMEM)
     dma = pltpu.SemaphoreType.DMA
-    local = (LOCAL, KERNELS)
     by, bt, pack, turned, pv, pu = constants
     call = pl.pallas_call(
         functools.partial(kernel, tiles),
@@ -489,15 +541,16 @@
             pltpu.VMEM(turned.shape[1:], BF),
             pltpu.VMEM(pv.shape, BF),
             pltpu.VMEM(pu.shape, BF),
-            pltpu.VMEM((LOCAL * KERNELS * 2 * UR, VR), F32),
-            pltpu.VMEM((GROUP,) + local + (2, UR, VR), F32),
-            pltpu.VMEM((UR, VR), F32),
-            pltpu.VMEM((UR, VR), F32),
-            pltpu.VMEM((5, UR, VR), F32),
+            pltpu.VMEM((DEPTH * UR, 2 * VR), F32),
+            pltpu.VMEM((GROUP, EDGE + UR, VR), F32),
+            pltpu.VMEM((GROUP, DEPTH, 4, UR, VR), F32),
+            pltpu.VMEM((UH, VR), F32),
+            pltpu.VMEM((UH, VR), F32),
+            pltpu.VMEM((5, UH, VR), F32),
             pltpu.VMEM((4, 2, UH, VR), F32),
-            pltpu.VMEM((UR, VR), F32),
-            pltpu.VMEM((3, UR, VR), F32),
-            pltpu.VMEM((GROUP, UR, VR), F32),
+            pltpu.VMEM((UH, VR), F32),
+            pltpu.VMEM((3, UH, VR), F32),
+            pltpu.VMEM((GROUP, UH, VR), F32),
             pltpu.VMEM((4, 2, UH, VR), F32),
             pltpu.VMEM((GROUP, LOCAL * KERNELS * 2 * ROWS, TP), F32),
             pltpu.VMEM((GROUP, LOCAL, ROWS, TP), F32),

time: 34.9 us -> 31.6 us (0.905)
  Pallas kernels: 32.8 us -> 29.7 us
    pallas_call x1, Pallas kernels: 32.8 us -> 29.7 us  [shards(): call(theta, target, kernel_real, kernel_imag, weights, thresholds, *(jnp....]
where the time goes in v2:
time: 31.6 us; the launch traced here: 31.4 us
  Pallas kernels  29.7 us (94%)
  local copies, waits for them, and re-layouts  1.67 us (5%)
    pallas_call x1, Pallas kernels, shards(): call(theta, target, kernel_real, kernel_imag, weights, thresholds, *(jnp....  29.7 us
    unnamed x1, local copies, waits for them, and re-layouts  1.67 us

profile of v2, /device:TPU:2, one launch (start us, length us, event | category | flops | bytes accessed | tf_op | source)
XLA Modules:
  0.0 31.4 jit_solution(18397074430134217701)
XLA Ops:
  0.0 29.7 %window_gradient.1 = f32[128,512]{1,0:T(8,128)} custom-call(f32[128,512]{1,0:T(8,128)} %theta_h.1, s32[512,512]{1,0:T(8,128)} %target_h.1, f32[2,65,2,65]{3,2,1,0:T(2,128)} %bitcast.2, f32[2,65,2,65]{3,2,1,0:T(2,128)} %bitcast.3, s32[8]{0:T(128)} %weights_s.1, f32[2]{0:T(128)} %thresholds_s.1, bf16[512,256]{1,0:T(8,128)(2,1)} %constant.12.clone.by_h, ...), custom_call_target="tpu_custom_call" | custom-call | tf_op jit(solution)/shard_map/window_gradient/pallas_call | solution.py:576
  29.7 1.7 %copy.14 = f32[128,512]{1,0:T(8,128)} copy(f32[128,512]{1,0:T(8,128)} %window_gradient.1) | data formatting | bytes 524288

commit v3 on v2

--- a/solution.py
+++ b/solution.py
@@ -128,11 +128,11 @@
 
 def kernel(
     tiles,
-    theta_h, target_h, kr_h, ki_h, weights_s, thresholds_s, by_h, bt_h, pack_h, turned_h, pv_h, pu_h,
-    out_h,
-    theta_v, target_v, raw_v, by, bt, pack, turned, pv, pu,
-    stack, zbuf, coef, rown, rhalo, rin, rsum, aown, ain, anear, jbuf, amps, resists, band, wanted, grad_v,
-    load_sem, zs_sem, zr_sem, rs_sem, rr_sem, hs_sem, hr_sem, as_sem, ar_sem, near_sem, out_sem,
+    theta_h, target_h, kr_h, ki_h, weights_h, thresholds_h, by_h, bt_h, pack_h, turned_h, pv_h, pu_h,
+    out_v,
+    weights_s, thresholds_s, theta_v, target_v, raw_v, by, bt, pack, turned, pv, pu,
+    stack, zbuf, coef, rown, rhalo, rin, rsum, aown, ain, anear, jbuf, amps, resists, band, wanted, factor,
+    load_sem, zs_sem, zr_sem, rs_sem, rr_sem, hs_sem, hr_sem, as_sem, ar_sem, near_sem,
 ):
     t = lax.axis_index("tile")
     c = lax.axis_index("cond")
@@ -153,11 +153,13 @@
     load_ki = load(ki_h, raw_v.at[1])
     load_pv = load(pv_h, pv)
     load_pu = load(pu_h, pu)
+    load_thresholds = load(thresholds_h, thresholds_s)
     load_theta = load(theta_h, theta_v)
     load_by = load(by_h, by)
     load_turned = load(turned_h.at[c], turned)
     load_pack = load(pack_h.at[c], pack)
     load_bt = load(bt_h, bt)
+    load_weights = load(weights_h, weights_s)
     load_target = load(target_h.at[pl.ds(pl.multiple_of(c * ROWS, ROWS), ROWS), :], target_v)
 
     def partner(mask):
@@ -172,14 +174,14 @@
     for mask in range(1, GROUP):
         greet(partner(mask))
     greet(mirror)
-    for other in range(GROUP):
-        @pl.when(has_next & (final | (other == 0)))
-        def _(other=other):
-            greet((t + 1, other))
-
-        @pl.when(has_prev & (first | (other == GROUP - 1)))
-        def _(other=other):
-            greet((t - 1, other))
+
+    @pl.when(has_next)
+    def _():
+        greet((t + 1, 0))
+
+    @pl.when(has_prev)
+    def _():
+        greet((t - 1, GROUP - 1))
 
     lane = lax.broadcasted_iota(jnp.int32, (UH, VR), 1)
     row = lax.broadcasted_iota(jnp.int32, (UH, VR), 0)
@@ -238,6 +240,7 @@
         value = value[:, VR:]
         edge = value if n == 0 else edge + pltpu.roll(value, 2 * n, 1)
     zbuf[0, EDGE:, :] = edge
+    load_thresholds.wait()
     for l in range(LOCAL):
         zbuf[0, EDGE + SPARE + l : EDGE + SPARE + l + 1, :] = jnp.full((1, VR), thresholds_s[l], F32)
 
@@ -253,9 +256,8 @@
     rown[...] = packed(both[:UR] + both[UR : 2 * UR])
     rhalo[...] = packed(both[2 * UR : 3 * UR] + both[3 * UR :])
 
-    across_next = jnp.where(final, GROUP, 1) * has_next.astype(jnp.int32)
-    across_prev = jnp.where(first, GROUP, 1) * has_prev.astype(jnp.int32)
-    pl.semaphore_wait(barrier, GROUP + across_next + across_prev)
+    edge_of = (has_next & final) | (has_prev & first)
+    pl.semaphore_wait(barrier, jnp.where(edge_of, 2 * GROUP, GROUP))
 
     def remote(src, dst, send, recv, device):
         return pltpu.make_async_remote_copy(
@@ -385,6 +387,7 @@
     lax.fori_loop(0, GROUP, forward, 0)
 
     load_target.wait()
+    load_weights.wait()
     weight_sum = weights_s[0]
     for n in range(1, CONDS):
         weight_sum = weight_sum + weights_s[n]
@@ -473,7 +476,6 @@
     def _():
         anear[...] = jnp.zeros_like(anear)
 
-    factor = grad_v
     factor[...] = (MASK_STEEP / (SIZE * SIZE)) * (1.0 - jnp.square(jnp.tanh(MASK_STEEP * theta_v[...])))
 
     for mask in range(1, GROUP):
@@ -490,9 +492,7 @@
         rows += [hi, hi, lo, jnp.zeros((256 - 3 * UR, VR), BF)]
     tall = dot(pack[...], jnp.concatenate(rows, axis=0))
     hi, lo = split(tall)
-    grad_v[...] = dot(jnp.concatenate([hi, lo, hi], axis=1), bt[...]) * factor[...]
-    out = pltpu.make_async_copy(grad_v, out_h, out_sem)
-    out.start()
+    out_v[...] = dot(jnp.concatenate([hi, lo, hi], axis=1), bt[...]) * factor[...]
 
     @pl.when(has_next & final)
     def _():
@@ -517,21 +517,19 @@
     def _():
         adjoint_next().wait_send()
 
-    out.wait()
-
 
 def shards(tiles, theta, target, kernel_real, kernel_imag, weights, thresholds):
     constants = tables()
-    anywhere = pl.BlockSpec(memory_space=pl.ANY)
-    scalars = pl.BlockSpec(memory_space=pltpu.SMEM)
     dma = pltpu.SemaphoreType.DMA
     by, bt, pack, turned, pv, pu = constants
     call = pl.pallas_call(
         functools.partial(kernel, tiles),
         out_shape=jax.ShapeDtypeStruct((ROWS, TP), F32),
-        in_specs=[anywhere] * 4 + [scalars] * 2 + [anywhere] * 6,
-        out_specs=anywhere,
+        in_specs=[pl.BlockSpec(memory_space=pltpu.HBM)] * 12,
+        out_specs=pl.BlockSpec(memory_space=pltpu.VMEM),
         scratch_shapes=[
+            pltpu.SMEM((CONDS,), jnp.int32),
+            pltpu.SMEM((LOCAL,), F32),
             pltpu.VMEM((ROWS, TP), F32),
             pltpu.VMEM((ROWS, TP), jnp.int32),
             pltpu.VMEM((2, LOCAL, KSUP, KERNELS, KSUP), F32),
@@ -557,7 +555,7 @@
             pltpu.VMEM((ROWS, TP), F32),
             pltpu.VMEM((ROWS, TP), F32),
             pltpu.VMEM((ROWS, TP), F32),
-            dma((10,)),
+            dma((12,)),
             dma((3,)),
             dma((3,)),
             dma((3,)),
@@ -567,13 +565,13 @@
             dma((5,)),
             dma((3,)),
             dma((4,)),
-            dma,
         ],
-        compiler_params=pltpu.CompilerParams(collective_id=0, has_side_effects=True),
+        compiler_params=pltpu.CompilerParams(collective_id=0, has_side_effects=True, vmem_limit_bytes=32 * 1024 * 1024),
         name="window_gradient",
     )
     kernel_real, kernel_imag = (jnp.swapaxes(x, 1, 2) for x in (kernel_real, kernel_imag))
-    return call(theta, target, kernel_real, kernel_imag, weights, thresholds, *(jnp.asarray(x) for x in constants))
+    arrays = (theta, target, kernel_real, kernel_imag, weights, thresholds, *(jnp.asarray(x) for x in constants))
+    return call(*(pltpu.with_memory_space_constraint(x, pltpu.HBM) for x in arrays))
 
 
 def solution(mesh):

time: 31.6 us -> 28.7 us (0.908)
  Pallas kernels: 29.7 us -> 27.9 us
  local copies, waits for them, and re-layouts: 1.67 us -> 0.71 us
    pallas_call x1, Pallas kernels: 29.7 us -> 27.9 us  [shards(): call(*(pltpu.with_memory_space_constraint(x, pltpu.HBM) for x in arrays))]
    unnamed x1, local copies, waits for them, and re-layouts: 1.67 us -> 0.71 us
where the time goes in v3:
time: 28.7 us; the launch traced here: 28.6 us
  Pallas kernels  27.9 us (97%)
  local copies, waits for them, and re-layouts  0.71 us (2%)
    pallas_call x1, Pallas kernels, shards(): call(*(pltpu.with_memory_space_constraint(x, pltpu.HBM) for x in arrays))  27.9 us
    unnamed x1, local copies, waits for them, and re-layouts  0.71 us

profile of v3, /device:TPU:2, one launch (start us, length us, event | category | flops | bytes accessed | tf_op | source)
XLA Modules:
  0.0 28.6 jit_solution(1482776977147384243)
XLA Ops:
  0.0 27.9 %window_gradient.1 = f32[128,512]{1,0:T(8,128)S(1)} custom-call(f32[128,512]{1,0:T(8,128)} %theta_h.1, s32[512,512]{1,0:T(8,128)} %target_h.1, f32[2,65,2,65]{3,2,1,0:T(2,128)} %bitcast.2, f32[2,65,2,65]{3,2,1,0:T(2,128)} %bitcast.3, s32[8]{0:T(128)} %weights_h.1, f32[2]{0:T(128)} %thresholds_h.1, bf16[512,256]{1,0:T(8,128)(2,1)} %constant.12.clone.by_h, ...), custom_call_target="tpu_custom_call" | custom-call | tf_op jit(solution)/shard_map/window_gradient/pallas_call | solution.py:574
  27.9 0.7 %copy.14 = f32[128,512]{1,0:T(8,128)} copy(f32[128,512]{1,0:T(8,128)S(1)} %window_gradient.1) | data formatting | bytes 524288

commit v4 on v3

--- a/solution.py
+++ b/solution.py
@@ -26,6 +26,7 @@
 FLAT = 2 * HALF
 DEPTH = LOCAL * KERNELS
 EDGE = DEPTH * UR
+GRID = 128
 SPARE = HALF + 1
 
 MASK_STEEP = 2.0
@@ -48,7 +49,7 @@
 
 
 def waves(positions):
-    phase = (np.asarray(positions)[:, None] * np.arange(HALF + 1)[None, :]) % SIZE
+    phase = np.fmod(np.asarray(positions, np.float64)[:, None] * np.arange(HALF + 1)[None, :], SIZE)
     angles = phase * (2.0 * math.pi / SIZE)
     return np.cos(angles), np.sin(angles)
 
@@ -97,6 +98,27 @@
     hi, lo = np_split(cols)
     by = np.concatenate([hi, lo], axis=1)
     bt = np.concatenate([hi.T, hi.T, lo.T], axis=0)
+    places = column_basis(np.arange(GRID) * (SIZE / GRID))
+    hi, lo = np_split(places.T)
+    zero = np.zeros_like(hi)
+    sample = np.concatenate([np.concatenate([hi, lo], axis=1), np.concatenate([hi, zero], axis=1)], axis=0)
+    hi, lo = np_split(places)
+    gather = np.concatenate([np.concatenate([hi, lo], axis=1), np.concatenate([hi, zero], axis=1)], axis=0)
+    phase = (np.arange(TP) + HALO) * (2.0 * math.pi / SIZE)
+    place = np.arange(GRID) * (2.0 * math.pi / GRID)
+    spread = np.ones((GRID, TP))
+    for f in range(1, GRID // 2):
+        spread += 2.0 * np.cos(f * (phase[None, :] - place[:, None]))
+    spread += np.cos(GRID // 2 * place)[:, None] * np.cos(GRID // 2 * phase)[None, :]
+    spread /= GRID
+    last = np.sin(GRID // 2 * phase)
+    hi, lo = np_split(spread)
+    last_hi, last_lo = np_split(last)
+    rest = np.zeros((VR, TP), bf)
+    rest[HALF - 1], rest[FLAT - 1], rest[FLAT + HALF - 1] = last_hi, last_lo, last_hi
+    fine = np.concatenate([hi, hi, lo, rest], axis=0)
+    coarse = np.concatenate([hi.T, lo.T], axis=1)
+    half_last = np.broadcast_to(0.5 * last, (8, TP)).astype(np.float32)
     pack = []
     turned = []
     for c in range(GROUP):
@@ -119,7 +141,7 @@
     pv = np.concatenate([pv, pv], axis=0)
     pu = parity_rows().astype(bf)
     pu = np.concatenate([pu, pu], axis=1)
-    return by, bt, np.stack(pack), np.stack(turned), pv, pu
+    return by, bt, np.stack(pack), np.stack(turned), pv, pu, sample, gather, fine, coarse, half_last
 
 
 def dot(a, b):
@@ -129,9 +151,10 @@
 def kernel(
     tiles,
     theta_h, target_h, kr_h, ki_h, weights_h, thresholds_h, by_h, bt_h, pack_h, turned_h, pv_h, pu_h,
+    sample_h, gather_h, fine_h, coarse_h, half_last_h,
     out_v,
     weights_s, thresholds_s, theta_v, target_v, raw_v, by, bt, pack, turned, pv, pu,
-    stack, zbuf, coef, rown, rhalo, rin, rsum, aown, ain, anear, jbuf, amps, resists, band, wanted, factor,
+    sample, gather, fine, coarse, half_last, stack, zbuf, coef, rown, rhalo, rin, rsum, aown, ain, anear, jbuf, amps, crossed, resists, band, wanted, factor,
     load_sem, zs_sem, zr_sem, rs_sem, rr_sem, hs_sem, hr_sem, as_sem, ar_sem, near_sem,
 ):
     t = lax.axis_index("tile")
@@ -158,6 +181,11 @@
     load_by = load(by_h, by)
     load_turned = load(turned_h.at[c], turned)
     load_pack = load(pack_h.at[c], pack)
+    load_sample = load(sample_h, sample)
+    load_fine = load(fine_h, fine)
+    load_coarse = load(coarse_h, coarse)
+    load_half = load(half_last_h, half_last)
+    load_gather = load(gather_h, gather)
     load_bt = load(bt_h, bt)
     load_weights = load(weights_h, weights_s)
     load_target = load(target_h.at[pl.ds(pl.multiple_of(c * ROWS, ROWS), ROWS), :], target_v)
@@ -329,7 +357,10 @@
         return [coef[s, n, 2 * ri + v, u * UH : (u + 1) * UH, :] for ri in range(2) for u in range(2) for v in range(2)]
 
     load_pack.wait()
-    load_bt.wait()
+    load_sample.wait()
+    load_fine.wait()
+    pair_lane = lax.broadcasted_iota(jnp.int32, (2 * ROWS, VR), 1)
+    block_lane = lax.broadcasted_iota(jnp.int32, (ROWS, VR), 1)
 
     def forward(s, carry):
         @pl.when(s == 2)
@@ -356,19 +387,35 @@
             hi, lo = split(grid)
             grids.append(jnp.concatenate([hi, hi, lo], axis=0))
         lhs = []
-        for grid in grids:
+        cross = []
+        for n, grid in enumerate(grids):
             tall = dot(pack[:, : 3 * UR], grid)
             tall = jnp.concatenate([tall[:, :VR], tall[:, VR:]], axis=0)
+            other = jnp.where(pair_lane == HALF - 1, pltpu.roll(tall, VR - HALF, 1), 0.0)
+            other = jnp.where(pair_lane == FLAT - 1, pltpu.roll(tall, HALF, 1), other)
+            crossed[s, n * 2 * ROWS : (n + 1) * 2 * ROWS, :] = other
+            other = tall * other
+            cross.append(other[:ROWS] + other[ROWS:])
             hi, lo = split(tall)
-            lhs.append(jnp.concatenate([hi, lo, hi], axis=1))
-        amp = dot(jnp.concatenate(lhs, axis=0), bt[...])
+            lhs.append(jnp.concatenate([hi, lo], axis=1))
+        amp = dot(jnp.concatenate(lhs, axis=0), sample[...])
+        amp = amp[:, :GRID] + amp[:, GRID:]
         amps[s] = amp
+        lhs = []
+        for l in range(LOCAL):
+            sampled = None
+            for part in range(4):
+                piece = amp[(l * 4 + part) * ROWS : (l * 4 + part + 1) * ROWS]
+                sampled = piece * piece if part == 0 else sampled + piece * piece
+            hi, lo = split(sampled)
+            edge = cross[2 * l] + cross[2 * l + 1]
+            near = edge.astype(BF).astype(F32)
+            edge = jnp.where(block_lane < FLAT, near, pltpu.roll(edge - near, FLAT, 1)).astype(BF)
+            lhs.append(jnp.concatenate([hi, lo, hi, edge], axis=1))
+        intensities = dot(jnp.concatenate(lhs, axis=0), fine[...])
         total = None
         for l in range(LOCAL):
-            intensity = None
-            for part in range(4):
-                piece = amp[(l * 4 + part) * ROWS : (l * 4 + part + 1) * ROWS]
-                intensity = piece * piece if part == 0 else intensity + piece * piece
+            intensity = intensities[l * ROWS : (l + 1) * ROWS]
             level = zbuf[s, EDGE + SPARE + l : EDGE + SPARE + l + 1, 0:1]
             resist = jax.nn.sigmoid(RESIST_STEEP * (intensity - level))
             resists[s, l] = resist
@@ -396,24 +443,40 @@
     wanted[...] = target_v[...].astype(F32)
     band[...] = band[...] * (4.0 * RESIST_STEEP * BAND_WEIGHT / CONDS / CONDS)
 
+    load_coarse.wait()
+    load_half.wait()
+    load_gather.wait()
+
     def backward(s, carry):
-        drives = []
+        fields = []
+        lasts = []
         for l in range(LOCAL):
             weight = jnp.full((8, TP), weights_s[(c ^ s) * LOCAL + l], jnp.int32).astype(F32) / weight_sum
             pull = (4.0 * RESIST_STEEP) * weight[0:1]
             resist = resists[s, l]
             slope = (pull + 4.0 * RESIST_STEEP * BAND_WEIGHT / CONDS) * resist - (pull * wanted[...] + band[...])
             field = slope * (resist - resist * resist)
+            lasts.append(jnp.sum(field * half_last[0:1, :], axis=1, keepdims=True))
+            fields.append(field)
+        hi, lo = split(jnp.concatenate(fields, axis=0))
+        wide = dot(jnp.concatenate([hi, lo], axis=0), coarse[...])
+        half = LOCAL * ROWS
+        push = wide[:half, :GRID] + wide[:half, GRID:] + wide[half:, :GRID]
+        drives = []
+        for l in range(LOCAL):
             for part in range(4):
                 at = (l * 4 + part) * ROWS
-                drives.append(field * amps[s, at : at + ROWS])
+                drives.append(push[l * ROWS : (l + 1) * ROWS] * amps[s, at : at + ROWS])
         hi, lo = split(jnp.concatenate(drives, axis=0))
-        wide = dot(jnp.concatenate([hi, lo], axis=0), by[...])
-        half = 8 * ROWS
-        drive = wide[:half, :VR] + wide[:half, VR:] + wide[half:, :VR]
+        drive = dot(jnp.concatenate([hi, lo], axis=1), gather[...])
+        drive = drive[:, :VR] + drive[:, VR:]
+        drives = []
+        for part in range(8):
+            at = part * ROWS
+            drives.append(drive[at : at + ROWS] + lasts[part // 4] * crossed[s, at : at + ROWS])
         sums = [[None, None] for _ in range(4)]
         for n in range(DEPTH):
-            pair = jnp.concatenate([drive[2 * n * ROWS : (2 * n + 1) * ROWS], drive[(2 * n + 1) * ROWS : (2 * n + 2) * ROWS]], axis=1)
+            pair = jnp.concatenate(drives[2 * n : 2 * n + 2], axis=1)
             hi, lo = split(pair)
             back = dot(turned[: 2 * UR, :], jnp.concatenate([hi, lo], axis=0))
             back = back[:UR] + back[UR:]
@@ -486,6 +549,7 @@
         for other in range(GROUP):
             adjoint_near(other).wait_recv()
 
+    load_bt.wait()
     rows = []
     for value in (aown[...] + ain[0] + ain[1] + ain[2], anear[0] + anear[1] + anear[2] + anear[3]):
         hi, lo = split(jnp.concatenate(unpacked(value), axis=0))
@@ -521,11 +585,11 @@
 def shards(tiles, theta, target, kernel_real, kernel_imag, weights, thresholds):
     constants = tables()
     dma = pltpu.SemaphoreType.DMA
-    by, bt, pack, turned, pv, pu = constants
+    by, bt, pack, turned, pv, pu, sample, gather, fine, coarse, half_last = constants
     call = pl.pallas_call(
         functools.partial(kernel, tiles),
         out_shape=jax.ShapeDtypeStruct((ROWS, TP), F32),
-        in_specs=[pl.BlockSpec(memory_space=pltpu.HBM)] * 12,
+        in_specs=[pl.BlockSpec(memory_space=pltpu.HBM)] * 17,
         out_specs=pl.BlockSpec(memory_space=pltpu.VMEM),
         scratch_shapes=[
             pltpu.SMEM((CONDS,), jnp.int32),
@@ -539,6 +603,11 @@
             pltpu.VMEM(turned.shape[1:], BF),
             pltpu.VMEM(pv.shape, BF),
             pltpu.VMEM(pu.shape, BF),
+            pltpu.VMEM(sample.shape, BF),
+            pltpu.VMEM(gather.shape, BF),
+            pltpu.VMEM(fine.shape, BF),
+            pltpu.VMEM(coarse.shape, BF),
+            pltpu.VMEM(half_last.shape, F32),
             pltpu.VMEM((DEPTH * UR, 2 * VR), F32),
             pltpu.VMEM((GROUP, EDGE + UR, VR), F32),
             pltpu.VMEM((GROUP, DEPTH, 4, UR, VR), F32),
@@ -550,12 +619,13 @@
             pltpu.VMEM((3, UH, VR), F32),
             pltpu.VMEM((GROUP, UH, VR), F32),
             pltpu.VMEM((4, 2, UH, VR), F32),
-            pltpu.VMEM((GROUP, LOCAL * KERNELS * 2 * ROWS, TP), F32),
+            pltpu.VMEM((GROUP, LOCAL * KERNELS * 2 * ROWS, GRID), F32),
+            pltpu.VMEM((GROUP, LOCAL * KERNELS * 2 * ROWS, VR), F32),
             pltpu.VMEM((GROUP, LOCAL, ROWS, TP), F32),
             pltpu.VMEM((ROWS, TP), F32),
             pltpu.VMEM((ROWS, TP), F32),
             pltpu.VMEM((ROWS, TP), F32),
-            dma((12,)),
+            dma((17,)),
             dma((3,)),
             dma((3,)),
             dma((3,)),

time: 28.7 us -> 28.9 us (level)
  no operation moved by 1% of the time
where the time goes in v4:
time: 28.9 us; the launch traced here: 28.7 us
  Pallas kernels  28 us (97%)
  local copies, waits for them, and re-layouts  0.71 us (2%)
    pallas_call x1, Pallas kernels, shards(): call(*(pltpu.with_memory_space_constraint(x, pltpu.HBM) for x in arrays))  28 us
    unnamed x1, local copies, waits for them, and re-layouts  0.71 us

profile of v4, /device:TPU:2, one launch (start us, length us, event | category | flops | bytes accessed | tf_op | source)
XLA Modules:
  0.0 28.7 jit_solution(11278740638615221086)
XLA Ops:
  0.0 28.0 %window_gradient.1 = f32[128,512]{1,0:T(8,128)S(1)} custom-call(f32[128,512]{1,0:T(8,128)} %theta_h.1, s32[512,512]{1,0:T(8,128)} %target_h.1, f32[2,65,2,65]{3,2,1,0:T(2,128)} %bitcast.2, f32[2,65,2,65]{3,2,1,0:T(2,128)} %bitcast.3, s32[8]{0:T(128)} %weights_h.1, f32[2]{0:T(128)} %thresholds_h.1, bf16[512,256]{1,0:T(8,128)(2,1)} %constant.22.clone.by_h, ...), custom_call_target="tpu_custom_call" | custom-call | tf_op jit(solution)/shard_map/window_gradient/pallas_call | solution.py:644
  28.0 0.7 %copy.19 = f32[128,512]{1,0:T(8,128)} copy(f32[128,512]{1,0:T(8,128)S(1)} %window_gradient.1) | data formatting | bytes 524288

commit v5 on v4

--- a/solution.py
+++ b/solution.py
@@ -97,7 +97,7 @@
     cols = column_basis(np.arange(TP) + HALO)
     hi, lo = np_split(cols)
     by = np.concatenate([hi, lo], axis=1)
-    bt = np.concatenate([hi.T, hi.T, lo.T], axis=0)
+    bt = np.concatenate([hi.T, lo.T], axis=0)
     places = column_basis(np.arange(GRID) * (SIZE / GRID))
     hi, lo = np_split(places.T)
     zero = np.zeros_like(hi)
@@ -116,7 +116,7 @@
     last_hi, last_lo = np_split(last)
     rest = np.zeros((VR, TP), bf)
     rest[HALF - 1], rest[FLAT - 1], rest[FLAT + HALF - 1] = last_hi, last_lo, last_hi
-    fine = np.concatenate([hi, hi, lo, rest], axis=0)
+    fine = np.concatenate([hi, lo, rest], axis=0)
     coarse = np.concatenate([hi.T, lo.T], axis=1)
     half_last = np.broadcast_to(0.5 * last, (8, TP)).astype(np.float32)
     pack = []
@@ -138,7 +138,6 @@
         pack.append(np.concatenate(row, axis=1))
         turned.append(np.concatenate(column, axis=0))
     pv = parity_columns().astype(bf)
-    pv = np.concatenate([pv, pv], axis=0)
     pu = parity_rows().astype(bf)
     pu = np.concatenate([pu, pu], axis=1)
     return by, bt, np.stack(pack), np.stack(turned), pv, pu, sample, gather, fine, coarse, half_last
@@ -154,7 +153,7 @@
     sample_h, gather_h, fine_h, coarse_h, half_last_h,
     out_v,
     weights_s, thresholds_s, theta_v, target_v, raw_v, by, bt, pack, turned, pv, pu,
-    sample, gather, fine, coarse, half_last, stack, zbuf, coef, rown, rhalo, rin, rsum, aown, ain, anear, jbuf, amps, crossed, resists, band, wanted, factor,
+    sample, gather, fine, coarse, half_last, stack, zbuf, coef, rown, rhalo, rin, rsum, aown, ain, anear, jbuf, amps, crossed, rows_v, edge_v, push_v, last_v, resists, band, wanted, factor,
     load_sem, zs_sem, zr_sem, rs_sem, rr_sem, hs_sem, hr_sem, as_sem, ar_sem, near_sem,
 ):
     t = lax.axis_index("tile")
@@ -174,7 +173,7 @@
 
     load_kr = load(kr_h, raw_v.at[0])
     load_ki = load(ki_h, raw_v.at[1])
-    load_pv = load(pv_h, pv)
+    load_pv = [load(pv_h, pv.at[pl.ds(at, 2 * VR), :]) for at in (0, 2 * VR)]
     load_pu = load(pu_h, pu)
     load_thresholds = load(thresholds_h, thresholds_s)
     load_theta = load(theta_h, theta_v)
@@ -182,11 +181,17 @@
     load_turned = load(turned_h.at[c], turned)
     load_pack = load(pack_h.at[c], pack)
     load_sample = load(sample_h, sample)
-    load_fine = load(fine_h, fine)
+    load_fine = [
+        load(fine_h.at[pl.ds(0, GRID), :], fine.at[pl.ds(0, GRID), :]),
+        load(fine_h, fine.at[pl.ds(GRID, 3 * GRID), :]),
+    ]
     load_coarse = load(coarse_h, coarse)
     load_half = load(half_last_h, half_last)
     load_gather = load(gather_h, gather)
-    load_bt = load(bt_h, bt)
+    load_bt = [
+        load(bt_h.at[pl.ds(0, VR), :], bt.at[pl.ds(0, VR), :]),
+        load(bt_h, bt.at[pl.ds(VR, 2 * VR), :]),
+    ]
     load_weights = load(weights_h, weights_s)
     load_target = load(target_h.at[pl.ds(pl.multiple_of(c * ROWS, ROWS), ROWS), :], target_v)
 
@@ -255,7 +260,8 @@
             for k in range(KERNELS):
                 at = (l * KERNELS + k) * UR
                 stack[at : at + KSUP, ri * VR : ri * VR + KSUP] = raw_v[ri, l, :, k, :]
-    load_pv.wait()
+    for copy in load_pv:
+        copy.wait()
     load_pu.wait()
     hi, lo = split(stack[...])
     folded = dot(jnp.concatenate([hi, lo], axis=1), pv[...])
@@ -358,22 +364,13 @@
 
     load_pack.wait()
     load_sample.wait()
-    load_fine.wait()
+    for copy in load_fine:
+        copy.wait()
     pair_lane = lax.broadcasted_iota(jnp.int32, (2 * ROWS, VR), 1)
     block_lane = lax.broadcasted_iota(jnp.int32, (ROWS, VR), 1)
 
-    def forward(s, carry):
-        @pl.when(s == 2)
-        def _():
-            kernels_to(2).wait_recv()
-            kernels_to(3).start()
-            unpack_kernels(2)
-
-        @pl.when(s == 3)
-        def _():
-            kernels_to(3).wait_recv()
-            unpack_kernels(3)
-
+    def grids_and_rows(s):
+        cross = []
         grids = []
         for n in range(DEPTH):
             ee_r, eo_r, oe_r, oo_r, ee_i, eo_i, oe_i, oo_i = parts_of(s, n)
@@ -386,19 +383,26 @@
             grid = jnp.concatenate([jnp.concatenate(real, axis=0), jnp.concatenate(imag, axis=0)], axis=1)
             hi, lo = split(grid)
             grids.append(jnp.concatenate([hi, hi, lo], axis=0))
-        lhs = []
-        cross = []
         for n, grid in enumerate(grids):
             tall = dot(pack[:, : 3 * UR], grid)
             tall = jnp.concatenate([tall[:, :VR], tall[:, VR:]], axis=0)
             other = jnp.where(pair_lane == HALF - 1, pltpu.roll(tall, VR - HALF, 1), 0.0)
             other = jnp.where(pair_lane == FLAT - 1, pltpu.roll(tall, HALF, 1), other)
-            crossed[s, n * 2 * ROWS : (n + 1) * 2 * ROWS, :] = other
+            at = n * 2 * ROWS
+            crossed[s, at : at + 2 * ROWS, :] = other
             other = tall * other
             cross.append(other[:ROWS] + other[ROWS:])
             hi, lo = split(tall)
-            lhs.append(jnp.concatenate([hi, lo], axis=1))
-        amp = dot(jnp.concatenate(lhs, axis=0), sample[...])
+            rows_v[s % 2, at : at + 2 * ROWS, :VR] = hi
+            rows_v[s % 2, at : at + 2 * ROWS, VR:] = lo
+        for l in range(LOCAL):
+            edge = cross[2 * l] + cross[2 * l + 1]
+            near = edge.astype(BF).astype(F32)
+            edge = jnp.where(block_lane < FLAT, near, pltpu.roll(edge - near, FLAT, 1)).astype(BF)
+            edge_v[s % 2, l * ROWS : (l + 1) * ROWS, :] = edge
+
+    def resist_of(s):
+        amp = dot(rows_v[s % 2], sample[...])
         amp = amp[:, :GRID] + amp[:, GRID:]
         amps[s] = amp
         lhs = []
@@ -408,10 +412,7 @@
                 piece = amp[(l * 4 + part) * ROWS : (l * 4 + part + 1) * ROWS]
                 sampled = piece * piece if part == 0 else sampled + piece * piece
             hi, lo = split(sampled)
-            edge = cross[2 * l] + cross[2 * l + 1]
-            near = edge.astype(BF).astype(F32)
-            edge = jnp.where(block_lane < FLAT, near, pltpu.roll(edge - near, FLAT, 1)).astype(BF)
-            lhs.append(jnp.concatenate([hi, lo, hi, edge], axis=1))
+            lhs.append(jnp.concatenate([hi, lo, hi, edge_v[s % 2, l * ROWS : (l + 1) * ROWS, :]], axis=1))
         intensities = dot(jnp.concatenate(lhs, axis=0), fine[...])
         total = None
         for l in range(LOCAL):
@@ -420,18 +421,24 @@
             resist = jax.nn.sigmoid(RESIST_STEEP * (intensity - level))
             resists[s, l] = resist
             total = resist if l == 0 else total + resist
-
-        @pl.when(s == 0)
-        def _():
+        if s == 0:
             band[...] = total
-
-        @pl.when(s > 0)
-        def _():
+        else:
             band[...] += total
 
-        return carry
-
-    lax.fori_loop(0, GROUP, forward, 0)
+    grids_and_rows(0)
+    kernels_to(2).wait_recv()
+    kernels_to(3).start()
+    unpack_kernels(2)
+    resist_of(0)
+    grids_and_rows(1)
+    resist_of(1)
+    grids_and_rows(2)
+    kernels_to(3).wait_recv()
+    unpack_kernels(3)
+    resist_of(2)
+    grids_and_rows(3)
+    resist_of(3)
 
     load_target.wait()
     load_weights.wait()
@@ -439,7 +446,6 @@
     for n in range(1, CONDS):
         weight_sum = weight_sum + weights_s[n]
     weight_sum = jnp.full((8, TP), weight_sum, jnp.int32).astype(F32)
-    jbuf[...] = jnp.zeros_like(jbuf)
     wanted[...] = target_v[...].astype(F32)
     band[...] = band[...] * (4.0 * RESIST_STEEP * BAND_WEIGHT / CONDS / CONDS)
 
@@ -447,33 +453,36 @@
     load_half.wait()
     load_gather.wait()
 
-    def backward(s, carry):
+    def push_of(s):
         fields = []
-        lasts = []
         for l in range(LOCAL):
             weight = jnp.full((8, TP), weights_s[(c ^ s) * LOCAL + l], jnp.int32).astype(F32) / weight_sum
             pull = (4.0 * RESIST_STEEP) * weight[0:1]
             resist = resists[s, l]
             slope = (pull + 4.0 * RESIST_STEEP * BAND_WEIGHT / CONDS) * resist - (pull * wanted[...] + band[...])
             field = slope * (resist - resist * resist)
-            lasts.append(jnp.sum(field * half_last[0:1, :], axis=1, keepdims=True))
+            last = jnp.sum(field * half_last[0:1, :], axis=1, keepdims=True)
+            last_v[s % 2, l * ROWS : (l + 1) * ROWS, :] = jnp.broadcast_to(last, (ROWS, VR))
             fields.append(field)
         hi, lo = split(jnp.concatenate(fields, axis=0))
         wide = dot(jnp.concatenate([hi, lo], axis=0), coarse[...])
         half = LOCAL * ROWS
-        push = wide[:half, :GRID] + wide[:half, GRID:] + wide[half:, :GRID]
+        push_v[s % 2] = wide[:half, :GRID] + wide[:half, GRID:] + wide[half:, :GRID]
+
+    def adjoint_of(s):
         drives = []
         for l in range(LOCAL):
             for part in range(4):
                 at = (l * 4 + part) * ROWS
-                drives.append(push[l * ROWS : (l + 1) * ROWS] * amps[s, at : at + ROWS])
+                drives.append(push_v[s % 2, l * ROWS : (l + 1) * ROWS, :] * amps[s, at : at + ROWS])
         hi, lo = split(jnp.concatenate(drives, axis=0))
         drive = dot(jnp.concatenate([hi, lo], axis=1), gather[...])
         drive = drive[:, :VR] + drive[:, VR:]
         drives = []
         for part in range(8):
             at = part * ROWS
-            drives.append(drive[at : at + ROWS] + lasts[part // 4] * crossed[s, at : at + ROWS])
+            last = last_v[s % 2, part // 4 * ROWS : (part // 4 + 1) * ROWS, :]
+            drives.append(drive[at : at + ROWS] + last * crossed[s, at : at + ROWS])
         sums = [[None, None] for _ in range(4)]
         for n in range(DEPTH):
             pair = jnp.concatenate(drives[2 * n : 2 * n + 2], axis=1)
@@ -494,10 +503,16 @@
                     sums[m][h] = term if n == 0 else sums[m][h] + term
         for m in range(4):
             for h in range(2):
-                jbuf[m, h] += sums[m][h]
-        return carry
-
-    lax.fori_loop(0, GROUP, backward, 0)
+                if s == 0:
+                    jbuf[m, h] = sums[m][h]
+                else:
+                    jbuf[m, h] += sums[m][h]
+
+    push_of(0)
+    for s in range(1, GROUP):
+        adjoint_of(s - 1)
+        push_of(s)
+    adjoint_of(GROUP - 1)
 
     halves = []
     for h in range(2):
@@ -549,7 +564,8 @@
         for other in range(GROUP):
             adjoint_near(other).wait_recv()
 
-    load_bt.wait()
+    for copy in load_bt:
+        copy.wait()
     rows = []
     for value in (aown[...] + ain[0] + ain[1] + ain[2], anear[0] + anear[1] + anear[2] + anear[3]):
         hi, lo = split(jnp.concatenate(unpacked(value), axis=0))
@@ -598,14 +614,14 @@
             pltpu.VMEM((ROWS, TP), jnp.int32),
             pltpu.VMEM((2, LOCAL, KSUP, KERNELS, KSUP), F32),
             pltpu.VMEM(by.shape, BF),
-            pltpu.VMEM(bt.shape, BF),
+            pltpu.VMEM((3 * VR, TP), BF),
             pltpu.VMEM(pack.shape[1:], BF),
             pltpu.VMEM(turned.shape[1:], BF),
-            pltpu.VMEM(pv.shape, BF),
+            pltpu.VMEM((4 * VR, 2 * VR), BF),
             pltpu.VMEM(pu.shape, BF),
             pltpu.VMEM(sample.shape, BF),
             pltpu.VMEM(gather.shape, BF),
-            pltpu.VMEM(fine.shape, BF),
+            pltpu.VMEM((4 * GRID, TP), BF),
             pltpu.VMEM(coarse.shape, BF),
             pltpu.VMEM(half_last.shape, F32),
             pltpu.VMEM((DEPTH * UR, 2 * VR), F32),
@@ -621,11 +637,15 @@
             pltpu.VMEM((4, 2, UH, VR), F32),
             pltpu.VMEM((GROUP, LOCAL * KERNELS * 2 * ROWS, GRID), F32),
             pltpu.VMEM((GROUP, LOCAL * KERNELS * 2 * ROWS, VR), F32),
+            pltpu.VMEM((2, LOCAL * KERNELS * 2 * ROWS, 2 * VR), BF),
+            pltpu.VMEM((2, LOCAL * ROWS, VR), BF),
+            pltpu.VMEM((2, LOCAL * ROWS, GRID), F32),
+            pltpu.VMEM((2, LOCAL * ROWS, VR), F32),
             pltpu.VMEM((GROUP, LOCAL, ROWS, TP), F32),
             pltpu.VMEM((ROWS, TP), F32),
             pltpu.VMEM((ROWS, TP), F32),
             pltpu.VMEM((ROWS, TP), F32),
-            dma((17,)),
+            dma((20,)),
             dma((3,)),
             dma((3,)),
             dma((3,)),

time: 28.9 us -> 28.2 us (0.976)
  Pallas kernels: 28 us -> 27.4 us
    pallas_call x1, Pallas kernels: 28 us -> 27.4 us  [shards(): call(*(pltpu.with_memory_space_constraint(x, pltpu.HBM) for x in arrays))]
where the time goes in v5:
time: 28.2 us; the launch traced here: 28.1 us
  Pallas kernels  27.4 us (97%)
  local copies, waits for them, and re-layouts  0.71 us (3%)
    pallas_call x1, Pallas kernels, shards(): call(*(pltpu.with_memory_space_constraint(x, pltpu.HBM) for x in arrays))  27.4 us
    unnamed x1, local copies, waits for them, and re-layouts  0.71 us

profile of v5, /device:TPU:2, one launch (start us, length us, event | category | flops | bytes accessed | tf_op | source)
XLA Modules:
  0.0 28.1 jit_solution(14697733112275723371)
XLA Ops:
  0.0 27.4 %window_gradient.1 = f32[128,512]{1,0:T(8,128)S(1)} custom-call(f32[128,512]{1,0:T(8,128)} %theta_h.1, s32[512,512]{1,0:T(8,128)} %target_h.1, f32[2,65,2,65]{3,2,1,0:T(2,128)} %bitcast.2, f32[2,65,2,65]{3,2,1,0:T(2,128)} %bitcast.3, s32[8]{0:T(128)} %weights_h.1, f32[2]{0:T(128)} %thresholds_h.1, bf16[512,256]{1,0:T(8,128)(2,1)} %constant.22.clone.by_h, ...), custom_call_target="tpu_custom_call" | custom-call | tf_op jit(solution)/shard_map/window_gradient/pallas_call | solution.py:664
  27.4 0.7 %copy.19 = f32[128,512]{1,0:T(8,128)} copy(f32[128,512]{1,0:T(8,128)S(1)} %window_gradient.1) | data formatting | bytes 524288

commit v6 on v5

--- a/solution.py
+++ b/solution.py
@@ -25,7 +25,10 @@
 VR = 128
 FLAT = 2 * HALF
 DEPTH = LOCAL * KERNELS
-EDGE = DEPTH * UR
+USED = UH + HALF
+EDGE = 2 * DEPTH
+CHUNK = EDGE + DEPTH // 2 * USED
+WIRE = EDGE + DEPTH * USED
 GRID = 128
 SPARE = HALF + 1
 
@@ -57,8 +60,9 @@
 def row_basis(positions):
     cos, sin = waves(positions)
     out = np.zeros((len(positions), UR))
-    out[:, : HALF + 1] = cos
-    out[:, UH + 1 : UH + HALF + 1] = sin[:, 1:]
+    out[:, :HALF] = cos[:, 1:]
+    out[:, HALF] = 1.0
+    out[:, UH:USED] = sin[:, 1:]
     return out
 
 
@@ -73,10 +77,10 @@
 
 def parity_rows():
     out = np.zeros((UR, UR))
-    out[0, HALF] = 1.0
+    out[HALF, HALF] = 1.0
     for j in range(1, HALF + 1):
-        out[j, HALF + j] = out[j, HALF - j] = out[UH + j, HALF + j] = 1.0
-        out[UH + j, HALF - j] = -1.0
+        out[j - 1, HALF + j] = out[j - 1, HALF - j] = out[UH + j - 1, HALF + j] = 1.0
+        out[UH + j - 1, HALF - j] = -1.0
     return out
 
 
@@ -240,17 +244,17 @@
         return out
 
     def unpack_kernels(s):
-        edge = zbuf[s, EDGE:, :]
+        used_lane, used_diagonal = tall_lane[:USED], diagonal[:USED]
         for n in range(DEPTH):
-            p = zbuf[s, n * UR : (n + 1) * UR, :]
+            p = zbuf[s, EDGE + n * USED : EDGE + (n + 1) * USED, :]
             p32, p64, p96 = (pltpu.roll(p, shift, 1) for shift in (HALF, 2 * HALF, 3 * HALF))
-            first_half = tall_lane < HALF
             for at, (a, b) in enumerate(((p, p32), (p96, p), (p64, p96), (p32, p64))):
-                value = jnp.where(first_half, a, b)
+                value = jnp.where(used_lane < HALF, a, b)
                 if at % 2 == 0:
-                    flat = pltpu.roll(edge, FLAT - (2 * n + at // 2), 1)
-                    value = jnp.where(tall_lane == FLAT, flat, value)
-                coef[s, n, at] = value
+                    flat = zbuf[s, 2 * n + at // 2 : 2 * n + at // 2 + 1, :]
+                    flat = jnp.sum(jnp.where(used_diagonal, flat, 0.0), axis=1, keepdims=True)
+                    value = jnp.where(used_lane == FLAT, flat, value)
+                coef[s, n, at, :USED] = value
 
     stack[...] = jnp.zeros_like(stack)
     load_kr.wait()
@@ -266,17 +270,17 @@
     hi, lo = split(stack[...])
     folded = dot(jnp.concatenate([hi, lo], axis=1), pv[...])
     hi, lo = split(folded)
-    edge = None
+    coef[:, :, :, USED:, :] = jnp.zeros((GROUP, DEPTH, 4, UR - USED, VR), F32)
+    load_thresholds.wait()
     for n in range(DEPTH):
         rhs = jnp.concatenate([hi[n * UR : (n + 1) * UR], lo[n * UR : (n + 1) * UR]], axis=0)
         value = dot(pu[...], rhs)
-        zbuf[0, n * UR : (n + 1) * UR, :] = value[:, :VR]
-        value = value[:, VR:]
-        edge = value if n == 0 else edge + pltpu.roll(value, 2 * n, 1)
-    zbuf[0, EDGE:, :] = edge
-    load_thresholds.wait()
-    for l in range(LOCAL):
-        zbuf[0, EDGE + SPARE + l : EDGE + SPARE + l + 1, :] = jnp.full((1, VR), thresholds_s[l], F32)
+        zbuf[0, EDGE + n * USED : EDGE + (n + 1) * USED, :] = value[:USED, :VR]
+        for ri in range(2):
+            flat = jnp.sum(jnp.where(diagonal, value[:, VR + ri : VR + ri + 1], 0.0), axis=0, keepdims=True)
+            if 2 * n + ri < LOCAL:
+                flat = jnp.where(lane[:1] == VR - 1, thresholds_s[2 * n + ri], flat)
+            zbuf[0, 2 * n + ri : 2 * n + ri + 1, :] = flat
 
     load_theta.wait()
     load_by.wait()
@@ -307,10 +311,14 @@
     def part(mask):
         return remote(rown, rin.at[mask - 1], rs_sem.at[mask - 1], rr_sem.at[mask - 1], partner(mask))
 
-    def kernels_to(mask):
+    def kernels_to(mask, chunk):
         device = partner(1) if mask != 2 else mirror
         source = 2 if mask == 3 else 0
-        return remote(zbuf.at[source], zbuf.at[mask], zs_sem.at[mask - 1], zr_sem.at[mask - 1], device)
+        rows = pl.ds(0, CHUNK) if chunk == 0 else pl.ds(CHUNK, WIRE - CHUNK)
+        sem = 2 * (mask - 1) + chunk
+        return remote(
+            zbuf.at[source, rows, :], zbuf.at[mask, rows, :], zs_sem.at[sem], zr_sem.at[sem], device
+        )
 
     @pl.when(has_next & final)
     def _():
@@ -325,7 +333,8 @@
     for mask in range(1, GROUP):
         part(mask).start()
     for mask in (2, 1):
-        kernels_to(mask).start()
+        for chunk in range(2):
+            kernels_to(mask, chunk).start()
 
     @pl.when(jnp.logical_not(has_prev))
     def _():
@@ -336,7 +345,8 @@
         rin[4] = jnp.zeros((UH, VR), F32)
 
     unpack_kernels(0)
-    kernels_to(1).wait_recv()
+    for chunk in range(2):
+        kernels_to(1, chunk).wait_recv()
     unpack_kernels(1)
 
     @pl.when(has_prev)
@@ -417,7 +427,7 @@
         total = None
         for l in range(LOCAL):
             intensity = intensities[l * ROWS : (l + 1) * ROWS]
-            level = zbuf[s, EDGE + SPARE + l : EDGE + SPARE + l + 1, 0:1]
+            level = zbuf[s, l : l + 1, VR - 1 : VR]
             resist = jax.nn.sigmoid(RESIST_STEEP * (intensity - level))
             resists[s, l] = resist
             total = resist if l == 0 else total + resist
@@ -427,14 +437,17 @@
             band[...] += total
 
     grids_and_rows(0)
-    kernels_to(2).wait_recv()
-    kernels_to(3).start()
-    unpack_kernels(2)
+    kernels_to(2, 0).wait_recv()
+    kernels_to(3, 0).start()
     resist_of(0)
     grids_and_rows(1)
+    kernels_to(2, 1).wait_recv()
+    kernels_to(3, 1).start()
+    unpack_kernels(2)
     resist_of(1)
     grids_and_rows(2)
-    kernels_to(3).wait_recv()
+    for chunk in range(2):
+        kernels_to(3, chunk).wait_recv()
     unpack_kernels(3)
     resist_of(2)
     grids_and_rows(3)
@@ -586,7 +599,8 @@
 
     for mask in range(1, GROUP):
         part(mask).wait_send()
-        kernels_to(mask).wait_send()
+        for chunk in range(2):
+            kernels_to(mask, chunk).wait_send()
         adjoint_part(mask).wait_send()
 
     @pl.when(has_prev)
@@ -625,7 +639,7 @@
             pltpu.VMEM(coarse.shape, BF),
             pltpu.VMEM(half_last.shape, F32),
             pltpu.VMEM((DEPTH * UR, 2 * VR), F32),
-            pltpu.VMEM((GROUP, EDGE + UR, VR), F32),
+            pltpu.VMEM((GROUP, WIRE, VR), F32),
             pltpu.VMEM((GROUP, DEPTH, 4, UR, VR), F32),
             pltpu.VMEM((UH, VR), F32),
             pltpu.VMEM((UH, VR), F32),
@@ -646,8 +660,8 @@
             pltpu.VMEM((ROWS, TP), F32),
             pltpu.VMEM((ROWS, TP), F32),
             dma((20,)),
-            dma((3,)),
-            dma((3,)),
+            dma((6,)),
+            dma((6,)),
             dma((3,)),
             dma((3,)),
             dma((4,)),

time: 28.2 us -> 27.7 us (0.982)
  Pallas kernels: 27.4 us -> 26.9 us
    pallas_call x1, Pallas kernels: 27.4 us -> 26.9 us  [shards(): call(*(pltpu.with_memory_space_constraint(x, pltpu.HBM) for x in arrays))]
where the time goes in v6:
time: 27.7 us; the launch traced here: 27.6 us
  Pallas kernels  26.9 us (97%)
  local copies, waits for them, and re-layouts  0.71 us (3%)
    pallas_call x1, Pallas kernels, shards(): call(*(pltpu.with_memory_space_constraint(x, pltpu.HBM) for x in arrays))  26.9 us
    unnamed x1, local copies, waits for them, and re-layouts  0.71 us

profile of v6, /device:TPU:2, one launch (start us, length us, event | category | flops | bytes accessed | tf_op | source)
XLA Modules:
  0.0 27.6 jit_solution(17536891796686850262)
XLA Ops:
  0.0 26.9 %window_gradient.1 = f32[128,512]{1,0:T(8,128)S(1)} custom-call(f32[128,512]{1,0:T(8,128)} %theta_h.1, s32[512,512]{1,0:T(8,128)} %target_h.1, f32[2,65,2,65]{3,2,1,0:T(2,128)} %bitcast.2, f32[2,65,2,65]{3,2,1,0:T(2,128)} %bitcast.3, s32[8]{0:T(128)} %weights_h.1, f32[2]{0:T(128)} %thresholds_h.1, bf16[512,256]{1,0:T(8,128)(2,1)} %constant.22.clone.by_h, ...), custom_call_target="tpu_custom_call" | custom-call | tf_op jit(solution)/shard_map/window_gradient/pallas_call | solution.py:678
  26.9 0.7 %copy.19 = f32[128,512]{1,0:T(8,128)} copy(f32[128,512]{1,0:T(8,128)S(1)} %window_gradient.1) | data formatting | bytes 524288

commit v7 on v6

--- a/solution.py
+++ b/solution.py
@@ -103,11 +103,16 @@
     by = np.concatenate([hi, lo], axis=1)
     bt = np.concatenate([hi.T, lo.T], axis=0)
     places = column_basis(np.arange(GRID) * (SIZE / GRID))
-    hi, lo = np_split(places.T)
-    zero = np.zeros_like(hi)
-    sample = np.concatenate([np.concatenate([hi, lo], axis=1), np.concatenate([hi, zero], axis=1)], axis=0)
-    hi, lo = np_split(places)
-    gather = np.concatenate([np.concatenate([hi, lo], axis=1), np.concatenate([hi, zero], axis=1)], axis=0)
+    hi, lo = np_split(places[:, :FLAT])
+    sample = np.zeros((3 * VR, 2 * GRID), bf)
+    gather = np.zeros((4 * GRID, 2 * VR), bf)
+    for ri in range(2):
+        for block, part in enumerate((hi, hi, lo)):
+            at = block * VR + ri * FLAT
+            sample[at : at + FLAT, ri * GRID : (ri + 1) * GRID] = part.T
+        gather[ri * GRID : (ri + 1) * GRID, ri * FLAT : (ri + 1) * FLAT] = hi
+        gather[ri * GRID : (ri + 1) * GRID, VR + ri * FLAT : VR + (ri + 1) * FLAT] = lo
+        gather[(2 + ri) * GRID : (3 + ri) * GRID, ri * FLAT : (ri + 1) * FLAT] = hi
     phase = (np.arange(TP) + HALO) * (2.0 * math.pi / SIZE)
     place = np.arange(GRID) * (2.0 * math.pi / GRID)
     spread = np.ones((GRID, TP))
@@ -119,7 +124,8 @@
     hi, lo = np_split(spread)
     last_hi, last_lo = np_split(last)
     rest = np.zeros((VR, TP), bf)
-    rest[HALF - 1], rest[FLAT - 1], rest[FLAT + HALF - 1] = last_hi, last_lo, last_hi
+    for at in (0, FLAT):
+        rest[at + HALF - 2], rest[at + HALF - 1], rest[at + FLAT - 1] = last_hi, last_hi, last_lo
     fine = np.concatenate([hi, lo, rest], axis=0)
     coarse = np.concatenate([hi.T, lo.T], axis=1)
     half_last = np.broadcast_to(0.5 * last, (8, TP)).astype(np.float32)
@@ -157,7 +163,7 @@
     sample_h, gather_h, fine_h, coarse_h, half_last_h,
     out_v,
     weights_s, thresholds_s, theta_v, target_v, raw_v, by, bt, pack, turned, pv, pu,
-    sample, gather, fine, coarse, half_last, stack, zbuf, coef, rown, rhalo, rin, rsum, aown, ain, anear, jbuf, amps, crossed, rows_v, edge_v, push_v, last_v, resists, band, wanted, factor,
+    sample, gather, fine, coarse, half_last, stack, zbuf, coef, ecoef, rown, rhalo, rin, rsum, erow, aown, ain, anear, jbuf, jflat, amps, crossed, rows_v, flat_v, edge_v, push_v, last_v, resists, band, wanted, factor,
     load_sem, zs_sem, zr_sem, rs_sem, rr_sem, hs_sem, hr_sem, as_sem, ar_sem, near_sem,
 ):
     t = lax.axis_index("tile")
@@ -224,11 +230,22 @@
     row = lax.broadcasted_iota(jnp.int32, (UH, VR), 0)
     tall_lane = lax.broadcasted_iota(jnp.int32, (UR, VR), 1)
     diagonal = tall_lane == lax.broadcasted_iota(jnp.int32, (UR, VR), 0)
-    sign_v = jnp.where((lane >= HALF) & (lane < FLAT), -1.0, 1.0).astype(F32)
+    odd = lane % FLAT >= HALF
+    sign_v = jnp.where(odd, -1.0, 1.0).astype(F32)
+    sign_i = jnp.where(lane >= FLAT, -1.0, 1.0).astype(F32)
+    edge_lane = lane[: 2 * DEPTH]
+    edge_row = row[: 2 * DEPTH]
 
     def swap(x):
-        out = jnp.where(lane < HALF, pltpu.roll(x, VR - HALF, 1), pltpu.roll(x, HALF, 1))
-        return jnp.where(lane < FLAT, out, 0.0)
+        return jnp.where(odd, pltpu.roll(x, HALF, 1), pltpu.roll(x, VR - HALF, 1))
+
+    def turned_edge(x):
+        out = jnp.where(edge_lane < UH, pltpu.roll(x, VR - UH, 1), -pltpu.roll(x, UH, 1))
+        return jnp.where(edge_lane < UR, out, 0.0)
+
+    def stacked(x):
+        near = x.astype(BF).astype(F32)
+        return jnp.concatenate([near, x - near], axis=0).astype(BF)
 
     def packed(x):
         out = jnp.where(lane < FLAT, x[:UH], pltpu.roll(x[UH:], FLAT, 1))
@@ -244,17 +261,23 @@
         return out
 
     def unpack_kernels(s):
-        used_lane, used_diagonal = tall_lane[:USED], diagonal[:USED]
         for n in range(DEPTH):
-            p = zbuf[s, EDGE + n * USED : EDGE + (n + 1) * USED, :]
-            p32, p64, p96 = (pltpu.roll(p, shift, 1) for shift in (HALF, 2 * HALF, 3 * HALF))
-            for at, (a, b) in enumerate(((p, p32), (p96, p), (p64, p96), (p32, p64))):
-                value = jnp.where(used_lane < HALF, a, b)
-                if at % 2 == 0:
-                    flat = zbuf[s, 2 * n + at // 2 : 2 * n + at // 2 + 1, :]
-                    flat = jnp.sum(jnp.where(used_diagonal, flat, 0.0), axis=1, keepdims=True)
-                    value = jnp.where(used_lane == FLAT, flat, value)
-                coef[s, n, at, :USED] = value
+            at = EDGE + n * USED
+            even = zbuf[s, at : at + UH, :]
+            uneven = zbuf[s, at + UH : at + USED, :]
+            odd_rows = odd[: USED - UH]
+            coef[s, n, 0] = jnp.where(odd, pltpu.roll(even, HALF, 1), even)
+            coef[s, n, 1] = jnp.where(odd, pltpu.roll(even, FLAT, 1), pltpu.roll(even, HALF, 1))
+            coef[s, n, 2, : USED - UH] = jnp.where(
+                odd_rows, pltpu.roll(uneven, VR - HALF, 1), pltpu.roll(uneven, FLAT, 1)
+            )
+            coef[s, n, 3, : USED - UH] = jnp.where(odd_rows, uneven, pltpu.roll(uneven, VR - HALF, 1))
+        flat = jnp.where(edge_lane < USED, zbuf[s, :EDGE, :], 0.0)
+        other = jnp.where(edge_row % 2 == 0, pltpu.roll(flat, EDGE - 1, 0), -pltpu.roll(flat, 1, 0))
+        ecoef[s, 0] = jnp.where(edge_lane < UH, flat, jnp.where(edge_lane < UR, pltpu.roll(flat, UH, 1), 0.0))
+        ecoef[s, 1] = jnp.where(
+            edge_lane < UH, pltpu.roll(other, VR - UH, 1), jnp.where(edge_lane < UR, other, 0.0)
+        )
 
     stack[...] = jnp.zeros_like(stack)
     load_kr.wait()
@@ -270,7 +293,7 @@
     hi, lo = split(stack[...])
     folded = dot(jnp.concatenate([hi, lo], axis=1), pv[...])
     hi, lo = split(folded)
-    coef[:, :, :, USED:, :] = jnp.zeros((GROUP, DEPTH, 4, UR - USED, VR), F32)
+    coef[:, :, 2:, USED - UH :, :] = jnp.zeros((GROUP, DEPTH, 2, UR - USED, VR), F32)
     load_thresholds.wait()
     for n in range(DEPTH):
         rhs = jnp.concatenate([hi[n * UR : (n + 1) * UR], lo[n * UR : (n + 1) * UR]], axis=0)
@@ -348,6 +371,10 @@
     for chunk in range(2):
         kernels_to(1, chunk).wait_recv()
     unpack_kernels(1)
+    for chunk in range(2):
+        kernels_to(2, chunk).wait_recv()
+        kernels_to(3, chunk).start()
+    unpack_kernels(2)
 
     @pl.when(has_prev)
     def _():
@@ -361,66 +388,73 @@
         part(mask).wait_recv()
 
     total = rown[...] + rin[0] + rin[1] + rin[2] + rin[3] + rin[4]
-    halves = unpacked(total * (1.0 / (SIZE * SIZE)))
+    total = total * (1.0 / (SIZE * SIZE))
+    keep = row < SPARE
+    turn = pltpu.roll(total, FLAT, 1)
+    halves = [
+        jnp.where(keep, jnp.where(lane < FLAT, total, turn), 0.0),
+        jnp.where(keep, jnp.where(lane < FLAT, turn, total), 0.0),
+    ]
     for h in range(2):
         sign_u = 1.0 - 2.0 * h
         rsum[0, h] = halves[h]
-        rsum[1, h] = sign_v * swap(halves[h])
-        rsum[2, h] = sign_u * halves[1 - h]
+        rsum[1, h] = sign_i * sign_v * swap(halves[h])
+        rsum[2, h] = sign_u * sign_i * halves[1 - h]
         rsum[3, h] = (-sign_u) * sign_v * swap(halves[1 - h])
-
-    def parts_of(s, n):
-        return [coef[s, n, 2 * ri + v, u * UH : (u + 1) * UH, :] for ri in range(2) for u in range(2) for v in range(2)]
+    flat = jnp.where(edge_lane < UR, total[SPARE : SPARE + 1], 0.0)
+    erow[0] = flat
+    erow[1] = turned_edge(flat)
 
     load_pack.wait()
     load_sample.wait()
     for copy in load_fine:
         copy.wait()
-    pair_lane = lax.broadcasted_iota(jnp.int32, (2 * ROWS, VR), 1)
     block_lane = lax.broadcasted_iota(jnp.int32, (ROWS, VR), 1)
 
     def grids_and_rows(s):
-        cross = []
         grids = []
         for n in range(DEPTH):
-            ee_r, eo_r, oe_r, oo_r, ee_i, eo_i, oe_i, oo_i = parts_of(s, n)
-            real = []
-            imag = []
+            grid = []
             for h in range(2):
-                r0, r1, r2, r3 = (rsum[m, h] for m in range(4))
-                real.append(ee_r * r0 + eo_i * r1 + oe_i * r2 + oo_r * r3)
-                imag.append(ee_i * r0 - eo_r * r1 - oe_r * r2 + oo_i * r3)
-            grid = jnp.concatenate([jnp.concatenate(real, axis=0), jnp.concatenate(imag, axis=0)], axis=1)
-            hi, lo = split(grid)
-            grids.append(jnp.concatenate([hi, hi, lo], axis=0))
-        for n, grid in enumerate(grids):
-            tall = dot(pack[:, : 3 * UR], grid)
-            tall = jnp.concatenate([tall[:, :VR], tall[:, VR:]], axis=0)
-            other = jnp.where(pair_lane == HALF - 1, pltpu.roll(tall, VR - HALF, 1), 0.0)
-            other = jnp.where(pair_lane == FLAT - 1, pltpu.roll(tall, HALF, 1), other)
-            at = n * 2 * ROWS
-            crossed[s, at : at + 2 * ROWS, :] = other
-            other = tall * other
-            cross.append(other[:ROWS] + other[ROWS:])
-            hi, lo = split(tall)
-            rows_v[s % 2, at : at + 2 * ROWS, :VR] = hi
-            rows_v[s % 2, at : at + 2 * ROWS, VR:] = lo
+                terms = [coef[s, n, m] * rsum[m, h] for m in range(4)]
+                grid.append((terms[0] + terms[1]) + (terms[2] + terms[3]))
+            grids.append(jnp.concatenate(grid, axis=0))
+        cross = [None] * LOCAL
         for l in range(LOCAL):
-            edge = cross[2 * l] + cross[2 * l + 1]
-            near = edge.astype(BF).astype(F32)
-            edge = jnp.where(block_lane < FLAT, near, pltpu.roll(edge - near, FLAT, 1)).astype(BF)
-            edge_v[s % 2, l * ROWS : (l + 1) * ROWS, :] = edge
+            hi, lo = split(jnp.concatenate(grids[KERNELS * l : KERNELS * (l + 1)], axis=1))
+            tall = dot(pack[:, : 3 * UR], jnp.concatenate([hi, hi, lo], axis=0))
+            for k in range(KERNELS):
+                part = tall[:, k * VR : (k + 1) * VR]
+                at = (l * KERNELS + k) * ROWS
+                other = jnp.where(block_lane % FLAT == HALF - 1, pltpu.roll(part, VR - HALF, 1), 0.0)
+                other = jnp.where(block_lane % FLAT == FLAT - 1, pltpu.roll(part, HALF, 1), other)
+                crossed[s, at : at + ROWS, :] = other
+                other = part * other
+                cross[l] = other if k == 0 else cross[l] + other
+                hi, lo = split(part)
+                rows_v[s % 2, at : at + ROWS, :VR] = hi
+                rows_v[s % 2, at : at + ROWS, VR:] = lo
+        for l in range(LOCAL):
+            near = cross[l].astype(BF).astype(F32)
+            far = pltpu.roll(cross[l] - near, VR - 1, 1)
+            edge_v[s % 2, l * ROWS : (l + 1) * ROWS, :] = jnp.where(block_lane % FLAT == HALF - 2, far, near).astype(BF)
+        flat = stacked(ecoef[s, 0] * erow[0] + ecoef[s, 1] * erow[1])
+        upper = dot(flat, turned[:VR, :ROWS])
+        lower = dot(flat, turned[UR : UR + VR, :ROWS])
+        flat_v[s % 2] = (upper[:EDGE] + upper[EDGE:] + lower[:EDGE]).T
 
     def resist_of(s):
-        amp = dot(rows_v[s % 2], sample[...])
-        amp = amp[:, :GRID] + amp[:, GRID:]
-        amps[s] = amp
+        amp = dot(jnp.concatenate([rows_v[s % 2], rows_v[s % 2, :, :VR]], axis=1), sample[...])
         lhs = []
         for l in range(LOCAL):
             sampled = None
-            for part in range(4):
-                piece = amp[(l * 4 + part) * ROWS : (l * 4 + part + 1) * ROWS]
-                sampled = piece * piece if part == 0 else sampled + piece * piece
+            for k in range(KERNELS):
+                n = l * KERNELS + k
+                for ri in range(2):
+                    piece = amp[n * ROWS : (n + 1) * ROWS, ri * GRID : (ri + 1) * GRID]
+                    piece = piece + flat_v[s % 2, :, 2 * n + ri : 2 * n + ri + 1]
+                    amps[s, n * ROWS : (n + 1) * ROWS, ri * GRID : (ri + 1) * GRID] = piece
+                    sampled = piece * piece if k + ri == 0 else sampled + piece * piece
             hi, lo = split(sampled)
             lhs.append(jnp.concatenate([hi, lo, hi, edge_v[s % 2, l * ROWS : (l + 1) * ROWS, :]], axis=1))
         intensities = dot(jnp.concatenate(lhs, axis=0), fine[...])
@@ -437,13 +471,8 @@
             band[...] += total
 
     grids_and_rows(0)
-    kernels_to(2, 0).wait_recv()
-    kernels_to(3, 0).start()
     resist_of(0)
     grids_and_rows(1)
-    kernels_to(2, 1).wait_recv()
-    kernels_to(3, 1).start()
-    unpack_kernels(2)
     resist_of(1)
     grids_and_rows(2)
     for chunk in range(2):
@@ -483,43 +512,50 @@
         push_v[s % 2] = wide[:half, :GRID] + wide[:half, GRID:] + wide[half:, :GRID]
 
     def adjoint_of(s):
-        drives = []
+        rows = []
+        flat = jnp.zeros((ROWS, VR), F32)
+        for n in range(DEPTH):
+            push = push_v[s % 2, n // KERNELS * ROWS : (n // KERNELS + 1) * ROWS, :]
+            drive = []
+            for ri in range(2):
+                piece = push * amps[s, n * ROWS : (n + 1) * ROWS, ri * GRID : (ri + 1) * GRID]
+                flat = jnp.where(block_lane == 2 * n + ri, jnp.sum(piece, axis=1, keepdims=True), flat)
+                drive.append(piece)
+            hi, lo = split(jnp.concatenate(drive, axis=1))
+            rows.append(jnp.concatenate([hi, lo], axis=1))
+        drive = dot(jnp.concatenate(rows, axis=0), gather[...])
+        drive = drive[:, :VR] + drive[:, VR:]
+        sums = [[None, None] for _ in range(4)]
         for l in range(LOCAL):
-            for part in range(4):
-                at = (l * 4 + part) * ROWS
-                drives.append(push_v[s % 2, l * ROWS : (l + 1) * ROWS, :] * amps[s, at : at + ROWS])
-        hi, lo = split(jnp.concatenate(drives, axis=0))
-        drive = dot(jnp.concatenate([hi, lo], axis=1), gather[...])
-        drive = drive[:, :VR] + drive[:, VR:]
-        drives = []
-        for part in range(8):
-            at = part * ROWS
-            last = last_v[s % 2, part // 4 * ROWS : (part // 4 + 1) * ROWS, :]
-            drives.append(drive[at : at + ROWS] + last * crossed[s, at : at + ROWS])
-        sums = [[None, None] for _ in range(4)]
-        for n in range(DEPTH):
-            pair = jnp.concatenate(drives[2 * n : 2 * n + 2], axis=1)
-            hi, lo = split(pair)
+            pair = []
+            for n in (KERNELS * l, KERNELS * l + 1):
+                last = last_v[s % 2, l * ROWS : (l + 1) * ROWS, :]
+                pair.append(drive[n * ROWS : (n + 1) * ROWS] + last * crossed[s, n * ROWS : (n + 1) * ROWS, :])
+            hi, lo = split(jnp.concatenate(pair, axis=1))
             back = dot(turned[: 2 * UR, :], jnp.concatenate([hi, lo], axis=0))
             back = back[:UR] + back[UR:]
-            ee_r, eo_r, oe_r, oo_r, ee_i, eo_i, oe_i, oo_i = parts_of(s, n)
-            for h in range(2):
-                qr = back[h * UH : (h + 1) * UH, :VR]
-                qi = back[h * UH : (h + 1) * UH, VR:]
-                terms = (
-                    ee_r * qr + ee_i * qi,
-                    eo_i * qr - eo_r * qi,
-                    oe_i * qr - oe_r * qi,
-                    oo_r * qr + oo_i * qi,
-                )
-                for m, term in enumerate(terms):
-                    sums[m][h] = term if n == 0 else sums[m][h] + term
+            for k in range(KERNELS):
+                for h in range(2):
+                    value = back[h * UH : (h + 1) * UH, k * VR : (k + 1) * VR]
+                    for m in range(4):
+                        term = coef[s, l * KERNELS + k, m] * value
+                        sums[m][h] = term if l + k == 0 else sums[m][h] + term
         for m in range(4):
             for h in range(2):
                 if s == 0:
                     jbuf[m, h] = sums[m][h]
                 else:
                     jbuf[m, h] += sums[m][h]
+        wide = dot(stacked(flat.T[:EDGE]), pack[:, : 2 * VR])
+        here = wide[:EDGE, :VR] + wide[EDGE:, :VR]
+        upper = pltpu.roll(wide[:EDGE, :VR], VR - UR, 1)
+        lower = pltpu.roll(wide[:EDGE, VR:], VR - UR, 1)
+        here = here + jnp.where(edge_lane < VR - UR, upper, lower)
+        term = ecoef[s, 0] * here - ecoef[s, 1] * turned_edge(here)
+        if s == 0:
+            jflat[...] = term
+        else:
+            jflat[...] += term
 
     push_of(0)
     for s in range(1, GROUP):
@@ -527,16 +563,21 @@
         push_of(s)
     adjoint_of(GROUP - 1)
 
+    def folded_part(m, h):
+        sign = 1.0 if m in (0, 3) else -1.0
+        return jbuf[m, h] + sign * pltpu.roll(jbuf[m, h], FLAT, 1)
+
     halves = []
     for h in range(2):
         sign_u = 1.0 - 2.0 * h
         halves.append(
-            jbuf[0, h]
-            + swap(sign_v * jbuf[1, h])
-            - sign_u * jbuf[2, 1 - h]
-            + swap(sign_u * sign_v * jbuf[3, 1 - h])
+            folded_part(0, h)
+            + swap(sign_v * folded_part(1, h))
+            - sign_u * folded_part(2, 1 - h)
+            + swap(sign_u * sign_v * folded_part(3, 1 - h))
         )
-    aown[...] = packed(jnp.concatenate(halves, axis=0))
+    value = jnp.where(lane < FLAT, halves[0], pltpu.roll(halves[1], FLAT, 1))
+    aown[...] = jnp.where(row == SPARE, jnp.sum(jflat[...], axis=0, keepdims=True), value)
 
     def adjoint_part(mask):
         return remote(aown, ain.at[mask - 1], as_sem.at[mask - 1], ar_sem.at[mask - 1], partner(mask))
@@ -640,18 +681,22 @@
             pltpu.VMEM(half_last.shape, F32),
             pltpu.VMEM((DEPTH * UR, 2 * VR), F32),
             pltpu.VMEM((GROUP, WIRE, VR), F32),
-            pltpu.VMEM((GROUP, DEPTH, 4, UR, VR), F32),
+            pltpu.VMEM((GROUP, DEPTH, 4, UH, VR), F32),
+            pltpu.VMEM((GROUP, 2, EDGE, VR), F32),
             pltpu.VMEM((UH, VR), F32),
             pltpu.VMEM((UH, VR), F32),
             pltpu.VMEM((5, UH, VR), F32),
             pltpu.VMEM((4, 2, UH, VR), F32),
+            pltpu.VMEM((2, EDGE, VR), F32),
             pltpu.VMEM((UH, VR), F32),
             pltpu.VMEM((3, UH, VR), F32),
             pltpu.VMEM((GROUP, UH, VR), F32),
             pltpu.VMEM((4, 2, UH, VR), F32),
-            pltpu.VMEM((GROUP, LOCAL * KERNELS * 2 * ROWS, GRID), F32),
-            pltpu.VMEM((GROUP, LOCAL * KERNELS * 2 * ROWS, VR), F32),
-            pltpu.VMEM((2, LOCAL * KERNELS * 2 * ROWS, 2 * VR), BF),
+            pltpu.VMEM((EDGE, VR), F32),
+            pltpu.VMEM((GROUP, DEPTH * ROWS, 2 * GRID), F32),
+            pltpu.VMEM((GROUP, DEPTH * ROWS, VR), F32),
+            pltpu.VMEM((2, DEPTH * ROWS, 2 * VR), BF),
+            pltpu.VMEM((2, ROWS, EDGE), F32),
             pltpu.VMEM((2, LOCAL * ROWS, VR), BF),
             pltpu.VMEM((2, LOCAL * ROWS, GRID), F32),
             pltpu.VMEM((2, LOCAL * ROWS, VR), F32),

time: 27.7 us -> 28 us (1.011)
  Pallas kernels: 26.9 us -> 27.2 us
where the time goes in v7:
time: 28 us; the launch traced here: 27.9 us
  Pallas kernels  27.2 us (97%)
  local copies, waits for them, and re-layouts  0.71 us (3%)
    pallas_call x1, Pallas kernels, shards(): call(*(pltpu.with_memory_space_constraint(x, pltpu.HBM) for x in arrays))  27.2 us
    unnamed x1, local copies, waits for them, and re-layouts  0.71 us

profile of v7, /device:TPU:2, one launch (start us, length us, event | category | flops | bytes accessed | tf_op | source)
XLA Modules:
  0.0 27.9 jit_solution(12132099422373760776)
XLA Ops:
  0.0 27.2 %window_gradient.1 = f32[128,512]{1,0:T(8,128)S(1)} custom-call(f32[128,512]{1,0:T(8,128)} %theta_h.1, s32[512,512]{1,0:T(8,128)} %target_h.1, f32[2,65,2,65]{3,2,1,0:T(2,128)} %bitcast.2, f32[2,65,2,65]{3,2,1,0:T(2,128)} %bitcast.3, s32[8]{0:T(128)} %weights_h.1, f32[2]{0:T(128)} %thresholds_h.1, bf16[512,256]{1,0:T(8,128)(2,1)} %constant.22.clone.by_h, ...), custom_call_target="tpu_custom_call" | custom-call | tf_op jit(solution)/shard_map/window_gradient/pallas_call | solution.py:723
  27.2 0.7 %copy.19 = f32[128,512]{1,0:T(8,128)} copy(f32[128,512]{1,0:T(8,128)S(1)} %window_gradient.1) | data formatting | bytes 524288

commit v8 on v7

--- a/solution.py
+++ b/solution.py
@@ -29,6 +29,7 @@
 EDGE = 2 * DEPTH
 CHUNK = EDGE + DEPTH // 2 * USED
 WIRE = EDGE + DEPTH * USED
+SPAN = DEPTH * ROWS
 GRID = 128
 SPARE = HALF + 1
 
@@ -371,10 +372,8 @@
     for chunk in range(2):
         kernels_to(1, chunk).wait_recv()
     unpack_kernels(1)
-    for chunk in range(2):
-        kernels_to(2, chunk).wait_recv()
-        kernels_to(3, chunk).start()
-    unpack_kernels(2)
+    kernels_to(2, 0).wait_recv()
+    kernels_to(3, 0).start()
 
     @pl.when(has_prev)
     def _():
@@ -432,55 +431,60 @@
                 other = part * other
                 cross[l] = other if k == 0 else cross[l] + other
                 hi, lo = split(part)
-                rows_v[s % 2, at : at + ROWS, :VR] = hi
-                rows_v[s % 2, at : at + ROWS, VR:] = lo
+                rows_v[s // 2, s % 2 * SPAN + at : s % 2 * SPAN + at + ROWS, :VR] = hi
+                rows_v[s // 2, s % 2 * SPAN + at : s % 2 * SPAN + at + ROWS, VR:] = lo
         for l in range(LOCAL):
             near = cross[l].astype(BF).astype(F32)
             far = pltpu.roll(cross[l] - near, VR - 1, 1)
-            edge_v[s % 2, l * ROWS : (l + 1) * ROWS, :] = jnp.where(block_lane % FLAT == HALF - 2, far, near).astype(BF)
+            edge_v[s, l * ROWS : (l + 1) * ROWS, :] = jnp.where(block_lane % FLAT == HALF - 2, far, near).astype(BF)
         flat = stacked(ecoef[s, 0] * erow[0] + ecoef[s, 1] * erow[1])
         upper = dot(flat, turned[:VR, :ROWS])
         lower = dot(flat, turned[UR : UR + VR, :ROWS])
-        flat_v[s % 2] = (upper[:EDGE] + upper[EDGE:] + lower[:EDGE]).T
-
-    def resist_of(s):
-        amp = dot(jnp.concatenate([rows_v[s % 2], rows_v[s % 2, :, :VR]], axis=1), sample[...])
+        flat_v[s] = (upper[:EDGE] + upper[EDGE:] + lower[:EDGE]).T
+
+    def resist_of(slots):
+        held = slots[0] // 2
+        amp = dot(jnp.concatenate([rows_v[held], rows_v[held, :, :VR]], axis=1), sample[...])
         lhs = []
-        for l in range(LOCAL):
-            sampled = None
-            for k in range(KERNELS):
-                n = l * KERNELS + k
-                for ri in range(2):
-                    piece = amp[n * ROWS : (n + 1) * ROWS, ri * GRID : (ri + 1) * GRID]
-                    piece = piece + flat_v[s % 2, :, 2 * n + ri : 2 * n + ri + 1]
-                    amps[s, n * ROWS : (n + 1) * ROWS, ri * GRID : (ri + 1) * GRID] = piece
-                    sampled = piece * piece if k + ri == 0 else sampled + piece * piece
-            hi, lo = split(sampled)
-            lhs.append(jnp.concatenate([hi, lo, hi, edge_v[s % 2, l * ROWS : (l + 1) * ROWS, :]], axis=1))
+        for s in slots:
+            for l in range(LOCAL):
+                sampled = None
+                for k in range(KERNELS):
+                    n = l * KERNELS + k
+                    at = s % 2 * SPAN + n * ROWS
+                    for ri in range(2):
+                        piece = amp[at : at + ROWS, ri * GRID : (ri + 1) * GRID]
+                        piece = piece + flat_v[s, :, 2 * n + ri : 2 * n + ri + 1]
+                        amps[s, n * ROWS : (n + 1) * ROWS, ri * GRID : (ri + 1) * GRID] = piece
+                        sampled = piece * piece if k + ri == 0 else sampled + piece * piece
+                hi, lo = split(sampled)
+                lhs.append(jnp.concatenate([hi, lo, hi, edge_v[s, l * ROWS : (l + 1) * ROWS, :]], axis=1))
         intensities = dot(jnp.concatenate(lhs, axis=0), fine[...])
         total = None
-        for l in range(LOCAL):
-            intensity = intensities[l * ROWS : (l + 1) * ROWS]
-            level = zbuf[s, l : l + 1, VR - 1 : VR]
-            resist = jax.nn.sigmoid(RESIST_STEEP * (intensity - level))
-            resists[s, l] = resist
-            total = resist if l == 0 else total + resist
-        if s == 0:
+        for s in slots:
+            for l in range(LOCAL):
+                at = (s % 2 * LOCAL + l) * ROWS
+                level = zbuf[s, l : l + 1, VR - 1 : VR]
+                resist = jax.nn.sigmoid(RESIST_STEEP * (intensities[at : at + ROWS] - level))
+                resists[s, l] = resist
+                total = resist if total is None else total + resist
+        if slots[0] == 0:
             band[...] = total
         else:
             band[...] += total
 
     grids_and_rows(0)
-    resist_of(0)
     grids_and_rows(1)
-    resist_of(1)
+    kernels_to(2, 1).wait_recv()
+    kernels_to(3, 1).start()
+    unpack_kernels(2)
+    resist_of((0, 1))
     grids_and_rows(2)
     for chunk in range(2):
         kernels_to(3, chunk).wait_recv()
     unpack_kernels(3)
-    resist_of(2)
     grids_and_rows(3)
-    resist_of(3)
+    resist_of((2, 3))
 
     load_target.wait()
     load_weights.wait()
@@ -495,73 +499,84 @@
     load_half.wait()
     load_gather.wait()
 
-    def push_of(s):
+    def push_of(slots):
         fields = []
-        for l in range(LOCAL):
-            weight = jnp.full((8, TP), weights_s[(c ^ s) * LOCAL + l], jnp.int32).astype(F32) / weight_sum
-            pull = (4.0 * RESIST_STEEP) * weight[0:1]
-            resist = resists[s, l]
-            slope = (pull + 4.0 * RESIST_STEEP * BAND_WEIGHT / CONDS) * resist - (pull * wanted[...] + band[...])
-            field = slope * (resist - resist * resist)
-            last = jnp.sum(field * half_last[0:1, :], axis=1, keepdims=True)
-            last_v[s % 2, l * ROWS : (l + 1) * ROWS, :] = jnp.broadcast_to(last, (ROWS, VR))
-            fields.append(field)
+        for s in slots:
+            for l in range(LOCAL):
+                weight = jnp.full((8, TP), weights_s[(c ^ s) * LOCAL + l], jnp.int32).astype(F32) / weight_sum
+                pull = (4.0 * RESIST_STEEP) * weight[0:1]
+                resist = resists[s, l]
+                slope = (pull + 4.0 * RESIST_STEEP * BAND_WEIGHT / CONDS) * resist - (pull * wanted[...] + band[...])
+                field = slope * (resist - resist * resist)
+                last = jnp.sum(field * half_last[0:1, :], axis=1, keepdims=True)
+                last_v[s, l * ROWS : (l + 1) * ROWS, :] = jnp.broadcast_to(last, (ROWS, VR))
+                fields.append(field)
         hi, lo = split(jnp.concatenate(fields, axis=0))
         wide = dot(jnp.concatenate([hi, lo], axis=0), coarse[...])
-        half = LOCAL * ROWS
-        push_v[s % 2] = wide[:half, :GRID] + wide[:half, GRID:] + wide[half:, :GRID]
-
-    def adjoint_of(s):
+        half = 2 * LOCAL * ROWS
+        push_v[slots[0] // 2] = wide[:half, :GRID] + wide[:half, GRID:] + wide[half:, :GRID]
+
+    def adjoint_of(slots):
         rows = []
-        flat = jnp.zeros((ROWS, VR), F32)
-        for n in range(DEPTH):
-            push = push_v[s % 2, n // KERNELS * ROWS : (n // KERNELS + 1) * ROWS, :]
-            drive = []
-            for ri in range(2):
-                piece = push * amps[s, n * ROWS : (n + 1) * ROWS, ri * GRID : (ri + 1) * GRID]
-                flat = jnp.where(block_lane == 2 * n + ri, jnp.sum(piece, axis=1, keepdims=True), flat)
-                drive.append(piece)
-            hi, lo = split(jnp.concatenate(drive, axis=1))
-            rows.append(jnp.concatenate([hi, lo], axis=1))
+        flats = []
+        for s in slots:
+            flat = []
+            for n in range(DEPTH):
+                at = (s % 2 * LOCAL + n // KERNELS) * ROWS
+                push = push_v[slots[0] // 2, at : at + ROWS, :]
+                drive = []
+                for ri in range(2):
+                    piece = push * amps[s, n * ROWS : (n + 1) * ROWS, ri * GRID : (ri + 1) * GRID]
+                    flat.append(jnp.where(block_lane == 2 * n + ri, jnp.sum(piece, axis=1, keepdims=True), 0.0))
+                    drive.append(piece)
+                hi, lo = split(jnp.concatenate(drive, axis=1))
+                rows.append(jnp.concatenate([hi, lo], axis=1))
+            while len(flat) > 1:
+                flat = [flat[i] + flat[i + 1] for i in range(0, len(flat), 2)]
+            flats.append(flat[0])
         drive = dot(jnp.concatenate(rows, axis=0), gather[...])
         drive = drive[:, :VR] + drive[:, VR:]
         sums = [[None, None] for _ in range(4)]
-        for l in range(LOCAL):
-            pair = []
-            for n in (KERNELS * l, KERNELS * l + 1):
-                last = last_v[s % 2, l * ROWS : (l + 1) * ROWS, :]
-                pair.append(drive[n * ROWS : (n + 1) * ROWS] + last * crossed[s, n * ROWS : (n + 1) * ROWS, :])
-            hi, lo = split(jnp.concatenate(pair, axis=1))
-            back = dot(turned[: 2 * UR, :], jnp.concatenate([hi, lo], axis=0))
-            back = back[:UR] + back[UR:]
-            for k in range(KERNELS):
-                for h in range(2):
-                    value = back[h * UH : (h + 1) * UH, k * VR : (k + 1) * VR]
-                    for m in range(4):
-                        term = coef[s, l * KERNELS + k, m] * value
-                        sums[m][h] = term if l + k == 0 else sums[m][h] + term
+        for s in slots:
+            for l in range(LOCAL):
+                pair = []
+                for n in (KERNELS * l, KERNELS * l + 1):
+                    at = s % 2 * SPAN + n * ROWS
+                    last = last_v[s, l * ROWS : (l + 1) * ROWS, :]
+                    pair.append(drive[at : at + ROWS] + last * crossed[s, n * ROWS : (n + 1) * ROWS, :])
+                hi, lo = split(jnp.concatenate(pair, axis=1))
+                back = dot(turned[: 2 * UR, :], jnp.concatenate([hi, lo], axis=0))
+                back = back[:UR] + back[UR:]
+                for k in range(KERNELS):
+                    for h in range(2):
+                        value = back[h * UH : (h + 1) * UH, k * VR : (k + 1) * VR]
+                        for m in range(4):
+                            term = coef[s, l * KERNELS + k, m] * value
+                            sums[m][h] = term if sums[m][h] is None else sums[m][h] + term
+        total = None
+        for s, flat in zip(slots, flats):
+            wide = dot(stacked(flat.T[:EDGE]), pack[:, : 2 * VR])
+            here = wide[:EDGE, :VR] + wide[EDGE:, :VR]
+            upper = pltpu.roll(wide[:EDGE, :VR], VR - UR, 1)
+            lower = pltpu.roll(wide[:EDGE, VR:], VR - UR, 1)
+            here = here + jnp.where(edge_lane < VR - UR, upper, lower)
+            term = ecoef[s, 0] * here - ecoef[s, 1] * turned_edge(here)
+            total = term if total is None else total + term
         for m in range(4):
             for h in range(2):
-                if s == 0:
+                if slots[0] == 0:
                     jbuf[m, h] = sums[m][h]
                 else:
                     jbuf[m, h] += sums[m][h]
-        wide = dot(stacked(flat.T[:EDGE]), pack[:, : 2 * VR])
-        here = wide[:EDGE, :VR] + wide[EDGE:, :VR]
-        upper = pltpu.roll(wide[:EDGE, :VR], VR - UR, 1)
-        lower = pltpu.roll(wide[:EDGE, VR:], VR - UR, 1)
-        here = here + jnp.where(edge_lane < VR - UR, upper, lower)
-        term = ecoef[s, 0] * here - ecoef[s, 1] * turned_edge(here)
-        if s == 0:
-            jflat[...] = term
+        if slots[0] == 0:
+            jflat[...] = total
         else:
-            jflat[...] += term
-
-    push_of(0)
-    for s in range(1, GROUP):
-        adjoint_of(s - 1)
-        push_of(s)
-    adjoint_of(GROUP - 1)
+            jflat[...] += total
+
+    push_of((0, 1))
+    adjoint_of((0, 1))
+    push_of((2, 3))
+    adjoint_of((2, 3))
 
     def folded_part(m, h):
         sign = 1.0 if m in (0, 3) else -1.0
@@ -695,11 +710,11 @@
             pltpu.VMEM((EDGE, VR), F32),
             pltpu.VMEM((GROUP, DEPTH * ROWS, 2 * GRID), F32),
             pltpu.VMEM((GROUP, DEPTH * ROWS, VR), F32),
-            pltpu.VMEM((2, DEPTH * ROWS, 2 * VR), BF),
-            pltpu.VMEM((2, ROWS, EDGE), F32),
-            pltpu.VMEM((2, LOCAL * ROWS, VR), BF),
-            pltpu.VMEM((2, LOCAL * ROWS, GRID), F32),
-            pltpu.VMEM((2, LOCAL * ROWS, VR), F32),
+            pltpu.VMEM((2, 2 * SPAN, 2 * VR), BF),
+            pltpu.VMEM((GROUP, ROWS, EDGE), F32),
+            pltpu.VMEM((GROUP, LOCAL * ROWS, VR), BF),
+            pltpu.VMEM((2, 2 * LOCAL * ROWS, GRID), F32),
+            pltpu.VMEM((GROUP, LOCAL * ROWS, VR), F32),
             pltpu.VMEM((GROUP, LOCAL, ROWS, TP), F32),
             pltpu.VMEM((ROWS, TP), F32),
             pltpu.VMEM((ROWS, TP), F32),

time: 28 us -> 26.8 us (0.957)
  Pallas kernels: 27.2 us -> 26 us
    pallas_call x1, Pallas kernels: 27.2 us -> 26 us  [shards(): call(*(pltpu.with_memory_space_constraint(x, pltpu.HBM) for x in arrays))]
where the time goes in v8:
time: 26.8 us; the launch traced here: 26.7 us
  Pallas kernels  26 us (97%)
  local copies, waits for them, and re-layouts  0.71 us (3%)
    pallas_call x1, Pallas kernels, shards(): call(*(pltpu.with_memory_space_constraint(x, pltpu.HBM) for x in arrays))  26 us
    unnamed x1, local copies, waits for them, and re-layouts  0.71 us

profile of v8, /device:TPU:2, one launch (start us, length us, event | category | flops | bytes accessed | tf_op | source)
XLA Modules:
  0.0 26.7 jit_solution(10804332508514465131)
XLA Ops:
  0.0 26.0 %window_gradient.1 = f32[128,512]{1,0:T(8,128)S(1)} custom-call(f32[128,512]{1,0:T(8,128)} %theta_h.1, s32[512,512]{1,0:T(8,128)} %target_h.1, f32[2,65,2,65]{3,2,1,0:T(2,128)} %bitcast.2, f32[2,65,2,65]{3,2,1,0:T(2,128)} %bitcast.3, s32[8]{0:T(128)} %weights_h.1, f32[2]{0:T(128)} %thresholds_h.1, bf16[512,256]{1,0:T(8,128)(2,1)} %constant.22.clone.by_h, ...), custom_call_target="tpu_custom_call" | custom-call | tf_op jit(solution)/shard_map/window_gradient/pallas_call | solution.py:738
  26.0 0.7 %copy.19 = f32[128,512]{1,0:T(8,128)} copy(f32[128,512]{1,0:T(8,128)S(1)} %window_gradient.1) | data formatting | bytes 524288

commit v9 on v8

--- a/solution.py
+++ b/solution.py
@@ -164,8 +164,8 @@
     sample_h, gather_h, fine_h, coarse_h, half_last_h,
     out_v,
     weights_s, thresholds_s, theta_v, target_v, raw_v, by, bt, pack, turned, pv, pu,
-    sample, gather, fine, coarse, half_last, stack, zbuf, coef, ecoef, rown, rhalo, rin, rsum, erow, aown, ain, anear, jbuf, jflat, amps, crossed, rows_v, flat_v, edge_v, push_v, last_v, resists, band, wanted, factor,
-    load_sem, zs_sem, zr_sem, rs_sem, rr_sem, hs_sem, hr_sem, as_sem, ar_sem, near_sem,
+    sample, gather, fine, coarse, half_last, stack, zbuf, coef, ecoef, passed, rown, rhalo, rin, rsum, erow, aown, ain, anear, jbuf, jflat, amps, crossed, rows_v, flat_v, edge_v, push_v, last_v, resists, band, wanted, factor,
+    load_sem, zs_sem, zr_sem, rs_sem, rr_sem, hs_sem, hr_sem, as_sem, ar_sem, near_sem, pass_sem,
 ):
     t = lax.axis_index("tile")
     c = lax.axis_index("cond")
@@ -219,13 +219,23 @@
         greet(partner(mask))
     greet(mirror)
 
+    bend = tiles // 2 - 1
+    via = (tiles - 4, 1)
+    at_bend = t == bend
+    after_bend = (t == bend + 1) & first
+    relays = (t == via[0]) & (c == via[1])
+
     @pl.when(has_next)
     def _():
-        greet((t + 1, 0))
+        greet((jnp.where(at_bend, via[0], t + 1), jnp.where(at_bend, via[1], 0)))
 
     @pl.when(has_prev)
     def _():
         greet((t - 1, GROUP - 1))
+
+    @pl.when(relays)
+    def _():
+        greet((bend + 1, 0))
 
     lane = lax.broadcasted_iota(jnp.int32, (UH, VR), 1)
     row = lax.broadcasted_iota(jnp.int32, (UH, VR), 0)
@@ -319,7 +329,8 @@
     rhalo[...] = packed(both[2 * UR : 3 * UR] + both[3 * UR :])
 
     edge_of = (has_next & final) | (has_prev & first)
-    pl.semaphore_wait(barrier, jnp.where(edge_of, 2 * GROUP, GROUP))
+    waited = jnp.where(edge_of | relays, 2 * GROUP, GROUP)
+    pl.semaphore_wait(barrier, jnp.where(after_bend, GROUP + 1, waited))
 
     def remote(src, dst, send, recv, device):
         return pltpu.make_async_remote_copy(
@@ -331,6 +342,12 @@
 
     def halo_prev(other):
         return remote(rhalo, rin.at[4], hs_sem.at[other], hr_sem.at[1], (t - 1, other))
+
+    def halo_via():
+        return remote(rhalo, passed, hs_sem.at[0], pass_sem, via)
+
+    def halo_passed(other):
+        return remote(passed, rin.at[4], hs_sem.at[other], hr_sem.at[1], (bend, other))
 
     def part(mask):
         return remote(rown, rin.at[mask - 1], rs_sem.at[mask - 1], rr_sem.at[mask - 1], partner(mask))
@@ -349,16 +366,26 @@
         for other in range(GROUP):
             halo_next(other).start()
 
-    @pl.when(has_prev & first)
+    @pl.when(has_prev & first & jnp.logical_not(after_bend))
     def _():
         for other in range(GROUP):
             halo_prev(other).start()
+
+    @pl.when(after_bend)
+    def _():
+        halo_via().start()
 
     for mask in range(1, GROUP):
         part(mask).start()
     for mask in (2, 1):
         for chunk in range(2):
             kernels_to(mask, chunk).start()
+
+    @pl.when(relays)
+    def _():
+        halo_via().wait_recv()
+        for other in range(GROUP):
+            halo_passed(other).start()
 
     @pl.when(jnp.logical_not(has_prev))
     def _():
@@ -648,10 +675,19 @@
         for other in range(GROUP):
             halo_next(other).wait_send()
 
-    @pl.when(has_prev & first)
+    @pl.when(has_prev & first & jnp.logical_not(after_bend))
     def _():
         for other in range(GROUP):
             halo_prev(other).wait_send()
+
+    @pl.when(after_bend)
+    def _():
+        halo_via().wait_send()
+
+    @pl.when(relays)
+    def _():
+        for other in range(GROUP):
+            halo_passed(other).wait_send()
 
     for mask in range(1, GROUP):
         part(mask).wait_send()
@@ -700,6 +736,7 @@
             pltpu.VMEM((GROUP, 2, EDGE, VR), F32),
             pltpu.VMEM((UH, VR), F32),
             pltpu.VMEM((UH, VR), F32),
+            pltpu.VMEM((UH, VR), F32),
             pltpu.VMEM((5, UH, VR), F32),
             pltpu.VMEM((4, 2, UH, VR), F32),
             pltpu.VMEM((2, EDGE, VR), F32),
@@ -729,6 +766,7 @@
             dma((5,)),
             dma((3,)),
             dma((4,)),
+            dma,
         ],
         compiler_params=pltpu.CompilerParams(collective_id=0, has_side_effects=True, vmem_limit_bytes=32 * 1024 * 1024),
         name="window_gradient",

time: 26.8 us -> 27 us (level)
  no operation moved by 1% of the time
where the time goes in v9:
time: 27 us; the launch traced here: 26.9 us
  Pallas kernels  26.1 us (97%)
  local copies, waits for them, and re-layouts  0.71 us (3%)
    pallas_call x1, Pallas kernels, shards(): call(*(pltpu.with_memory_space_constraint(x, pltpu.HBM) for x in arrays))  26.1 us
    unnamed x1, local copies, waits for them, and re-layouts  0.71 us

profile of v9, /device:TPU:2, one launch (start us, length us, event | category | flops | bytes accessed | tf_op | source)
XLA Modules:
  0.0 26.9 jit_solution(2742081583739978291)
XLA Ops:
  0.0 26.1 %window_gradient.1 = f32[128,512]{1,0:T(8,128)S(1)} custom-call(f32[128,512]{1,0:T(8,128)} %theta_h.1, s32[512,512]{1,0:T(8,128)} %target_h.1, f32[2,65,2,65]{3,2,1,0:T(2,128)} %bitcast.2, f32[2,65,2,65]{3,2,1,0:T(2,128)} %bitcast.3, s32[8]{0:T(128)} %weights_h.1, f32[2]{0:T(128)} %thresholds_h.1, bf16[512,256]{1,0:T(8,128)(2,1)} %constant.22.clone.by_h, ...), custom_call_target="tpu_custom_call" | custom-call | tf_op jit(solution)/shard_map/window_gradient/pallas_call | solution.py:776
  26.1 0.7 %copy.19 = f32[128,512]{1,0:T(8,128)} copy(f32[128,512]{1,0:T(8,128)S(1)} %window_gradient.1) | data formatting | bytes 524288

commit v10 on v9

--- a/solution.py
+++ b/solution.py
@@ -220,14 +220,14 @@
     greet(mirror)
 
     bend = tiles // 2 - 1
-    via = (tiles - 4, 1)
+    between = bend - 3
     at_bend = t == bend
     after_bend = (t == bend + 1) & first
-    relays = (t == via[0]) & (c == via[1])
+    relays = (t == between) & jnp.logical_not(first | final)
 
     @pl.when(has_next)
     def _():
-        greet((jnp.where(at_bend, via[0], t + 1), jnp.where(at_bend, via[1], 0)))
+        greet((jnp.where(at_bend, between, t + 1), jnp.where(at_bend, 1 + c // 2, 0)))
 
     @pl.when(has_prev)
     def _():
@@ -329,8 +329,8 @@
     rhalo[...] = packed(both[2 * UR : 3 * UR] + both[3 * UR :])
 
     edge_of = (has_next & final) | (has_prev & first)
-    waited = jnp.where(edge_of | relays, 2 * GROUP, GROUP)
-    pl.semaphore_wait(barrier, jnp.where(after_bend, GROUP + 1, waited))
+    waited = jnp.where(edge_of, 2 * GROUP, GROUP)
+    pl.semaphore_wait(barrier, jnp.where(after_bend | relays, GROUP + 2, waited))
 
     def remote(src, dst, send, recv, device):
         return pltpu.make_async_remote_copy(
@@ -343,11 +343,11 @@
     def halo_prev(other):
         return remote(rhalo, rin.at[4], hs_sem.at[other], hr_sem.at[1], (t - 1, other))
 
-    def halo_via():
-        return remote(rhalo, passed, hs_sem.at[0], pass_sem, via)
-
-    def halo_passed(other):
-        return remote(passed, rin.at[4], hs_sem.at[other], hr_sem.at[1], (bend, other))
+    def halo_via(side):
+        return remote(rhalo, passed, hs_sem.at[side], pass_sem, (between, 1 + side))
+
+    def halo_passed(core):
+        return remote(passed, rin.at[4], hs_sem.at[core], hr_sem.at[1], (bend, 2 * (c - 1) + core))
 
     def part(mask):
         return remote(rown, rin.at[mask - 1], rs_sem.at[mask - 1], rr_sem.at[mask - 1], partner(mask))
@@ -373,7 +373,8 @@
 
     @pl.when(after_bend)
     def _():
-        halo_via().start()
+        for side in range(2):
+            halo_via(side).start()
 
     for mask in range(1, GROUP):
         part(mask).start()
@@ -383,9 +384,9 @@
 
     @pl.when(relays)
     def _():
-        halo_via().wait_recv()
-        for other in range(GROUP):
-            halo_passed(other).start()
+        halo_via(0).wait_recv()
+        for core in range(2):
+            halo_passed(core).start()
 
     @pl.when(jnp.logical_not(has_prev))
     def _():
@@ -399,8 +400,6 @@
     for chunk in range(2):
         kernels_to(1, chunk).wait_recv()
     unpack_kernels(1)
-    kernels_to(2, 0).wait_recv()
-    kernels_to(3, 0).start()
 
     @pl.when(has_prev)
     def _():
@@ -502,10 +501,12 @@
 
     grids_and_rows(0)
     grids_and_rows(1)
+    kernels_to(2, 0).wait_recv()
+    kernels_to(3, 0).start()
+    resist_of((0, 1))
     kernels_to(2, 1).wait_recv()
     kernels_to(3, 1).start()
     unpack_kernels(2)
-    resist_of((0, 1))
     grids_and_rows(2)
     for chunk in range(2):
         kernels_to(3, chunk).wait_recv()
@@ -646,29 +647,28 @@
 
     near = (first & has_prev) | (final & has_next)
 
-    @pl.when(jnp.logical_not(near))
-    def _():
-        anear[...] = jnp.zeros_like(anear)
-
     factor[...] = (MASK_STEEP / (SIZE * SIZE)) * (1.0 - jnp.square(jnp.tanh(MASK_STEEP * theta_v[...])))
+    for copy in load_bt:
+        copy.wait()
 
     for mask in range(1, GROUP):
         adjoint_part(mask).wait_recv()
 
+    def sensitivity(value, rows, columns):
+        hi, lo = split(jnp.concatenate(unpacked(value), axis=0))
+        value = jnp.concatenate([hi, hi, lo, jnp.zeros((256 - 3 * UR, VR), BF)], axis=0)
+        hi, lo = split(dot(pack[rows, columns], value))
+        return dot(jnp.concatenate([hi, lo, hi], axis=1), bt[...])
+
+    out_v[...] = sensitivity(aown[...] + ain[0] + ain[1] + ain[2], slice(None), slice(0, 256)) * factor[...]
+
     @pl.when(near)
     def _():
         for other in range(GROUP):
             adjoint_near(other).wait_recv()
-
-    for copy in load_bt:
-        copy.wait()
-    rows = []
-    for value in (aown[...] + ain[0] + ain[1] + ain[2], anear[0] + anear[1] + anear[2] + anear[3]):
-        hi, lo = split(jnp.concatenate(unpacked(value), axis=0))
-        rows += [hi, hi, lo, jnp.zeros((256 - 3 * UR, VR), BF)]
-    tall = dot(pack[...], jnp.concatenate(rows, axis=0))
-    hi, lo = split(tall)
-    out_v[...] = dot(jnp.concatenate([hi, lo, hi], axis=1), bt[...]) * factor[...]
+        edge = pl.ds(pl.multiple_of(jnp.where(first, 0, ROWS - HALO), HALO), HALO)
+        value = anear[0] + anear[1] + anear[2] + anear[3]
+        out_v[edge, :] += sensitivity(value, edge, slice(256, 512)) * factor[edge, :]
 
     @pl.when(has_next & final)
     def _():
@@ -682,12 +682,13 @@
 
     @pl.when(after_bend)
     def _():
-        halo_via().wait_send()
+        for side in range(2):
+            halo_via(side).wait_send()
 
     @pl.when(relays)
     def _():
-        for other in range(GROUP):
-            halo_passed(other).wait_send()
+        for core in range(2):
+            halo_passed(core).wait_send()
 
     for mask in range(1, GROUP):
         part(mask).wait_send()

time: 27 us -> 27.2 us (level)
  Pallas kernels: 26.1 us -> 26.4 us
    pallas_call x1, Pallas kernels: 26.1 us -> 26.4 us  [shards(): call(*(pltpu.with_memory_space_constraint(x, pltpu.HBM) for x in arrays))]
where the time goes in v10:
time: 27.2 us; the launch traced here: 27.1 us
  Pallas kernels  26.4 us (97%)
  local copies, waits for them, and re-layouts  0.71 us (3%)
    pallas_call x1, Pallas kernels, shards(): call(*(pltpu.with_memory_space_constraint(x, pltpu.HBM) for x in arrays))  26.4 us
    unnamed x1, local copies, waits for them, and re-layouts  0.71 us

profile of v10, /device:TPU:2, one launch (start us, length us, event | category | flops | bytes accessed | tf_op | source)
XLA Modules:
  0.0 27.1 jit_solution(5078732911051379132)
XLA Ops:
  0.0 26.4 %window_gradient.1 = f32[128,512]{1,0:T(8,128)S(1)} custom-call(f32[128,512]{1,0:T(8,128)} %theta_h.1, s32[512,512]{1,0:T(8,128)} %target_h.1, f32[2,65,2,65]{3,2,1,0:T(2,128)} %bitcast.2, f32[2,65,2,65]{3,2,1,0:T(2,128)} %bitcast.3, s32[8]{0:T(128)} %weights_h.1, f32[2]{0:T(128)} %thresholds_h.1, bf16[512,256]{1,0:T(8,128)(2,1)} %constant.22.clone.by_h, ...), custom_call_target="tpu_custom_call" | custom-call | tf_op jit(solution)/shard_map/window_gradient/pallas_call | solution.py:777
  26.4 0.7 %copy.19 = f32[128,512]{1,0:T(8,128)} copy(f32[128,512]{1,0:T(8,128)S(1)} %window_gradient.1) | data formatting | bytes 524288

commit v11 on v10

--- a/solution.py
+++ b/solution.py
@@ -500,13 +500,13 @@
             band[...] += total
 
     grids_and_rows(0)
-    grids_and_rows(1)
     kernels_to(2, 0).wait_recv()
     kernels_to(3, 0).start()
-    resist_of((0, 1))
+    grids_and_rows(1)
     kernels_to(2, 1).wait_recv()
     kernels_to(3, 1).start()
     unpack_kernels(2)
+    resist_of((0, 1))
     grids_and_rows(2)
     for chunk in range(2):
         kernels_to(3, chunk).wait_recv()

time: 27.2 us -> 26.7 us (0.982)
  Pallas kernels: 26.4 us -> 25.8 us
    pallas_call x1, Pallas kernels: 26.4 us -> 25.8 us  [shards(): call(*(pltpu.with_memory_space_constraint(x, pltpu.HBM) for x in arrays))]
where the time goes in v11:
time: 26.7 us; the launch traced here: 26.6 us
  Pallas kernels  25.8 us (97%)
  local copies, waits for them, and re-layouts  0.71 us (3%)
    pallas_call x1, Pallas kernels, shards(): call(*(pltpu.with_memory_space_constraint(x, pltpu.HBM) for x in arrays))  25.8 us
    unnamed x1, local copies, waits for them, and re-layouts  0.71 us

profile of v11, /device:TPU:2, one launch (start us, length us, event | category | flops | bytes accessed | tf_op | source)
XLA Modules:
  0.0 26.6 jit_solution(12781682967021393378)
XLA Ops:
  0.0 25.8 %window_gradient.1 = f32[128,512]{1,0:T(8,128)S(1)} custom-call(f32[128,512]{1,0:T(8,128)} %theta_h.1, s32[512,512]{1,0:T(8,128)} %target_h.1, f32[2,65,2,65]{3,2,1,0:T(2,128)} %bitcast.2, f32[2,65,2,65]{3,2,1,0:T(2,128)} %bitcast.3, s32[8]{0:T(128)} %weights_h.1, f32[2]{0:T(128)} %thresholds_h.1, bf16[512,256]{1,0:T(8,128)(2,1)} %constant.22.clone.by_h, ...), custom_call_target="tpu_custom_call" | custom-call | tf_op jit(solution)/shard_map/window_gradient/pallas_call | solution.py:777
  25.9 0.7 %copy.19 = f32[128,512]{1,0:T(8,128)} copy(f32[128,512]{1,0:T(8,128)S(1)} %window_gradient.1) | data formatting | bytes 524288

commit v12 on v11

--- a/solution.py
+++ b/solution.py
@@ -220,7 +220,7 @@
     greet(mirror)
 
     bend = tiles // 2 - 1
-    between = bend - 3
+    between = bend - 12
     at_bend = t == bend
     after_bend = (t == bend + 1) & first
     relays = (t == between) & jnp.logical_not(first | final)

time: 26.7 us -> 26.5 us (level)
  no operation moved by 1% of the time
where the time goes in v12:
time: 26.5 us; the launch traced here: 26.4 us
  Pallas kernels  25.7 us (97%)
  local copies, waits for them, and re-layouts  0.71 us (3%)
    pallas_call x1, Pallas kernels, shards(): call(*(pltpu.with_memory_space_constraint(x, pltpu.HBM) for x in arrays))  25.7 us
    unnamed x1, local copies, waits for them, and re-layouts  0.71 us

profile of v12, /device:TPU:2, one launch (start us, length us, event | category | flops | bytes accessed | tf_op | source)
XLA Modules:
  0.0 26.4 jit_solution(9050547486978386548)
XLA Ops:
  0.0 25.7 %window_gradient.1 = f32[128,512]{1,0:T(8,128)S(1)} custom-call(f32[128,512]{1,0:T(8,128)} %theta_h.1, s32[512,512]{1,0:T(8,128)} %target_h.1, f32[2,65,2,65]{3,2,1,0:T(2,128)} %bitcast.2, f32[2,65,2,65]{3,2,1,0:T(2,128)} %bitcast.3, s32[8]{0:T(128)} %weights_h.1, f32[2]{0:T(128)} %thresholds_h.1, bf16[512,256]{1,0:T(8,128)(2,1)} %constant.22.clone.by_h, ...), custom_call_target="tpu_custom_call" | custom-call | tf_op jit(solution)/shard_map/window_gradient/pallas_call | solution.py:777
  25.7 0.7 %copy.19 = f32[128,512]{1,0:T(8,128)} copy(f32[128,512]{1,0:T(8,128)S(1)} %window_gradient.1) | data formatting | bytes 524288

commit v13 on v12

--- a/solution.py
+++ b/solution.py
@@ -164,7 +164,7 @@
     sample_h, gather_h, fine_h, coarse_h, half_last_h,
     out_v,
     weights_s, thresholds_s, theta_v, target_v, raw_v, by, bt, pack, turned, pv, pu,
-    sample, gather, fine, coarse, half_last, stack, zbuf, coef, ecoef, passed, rown, rhalo, rin, rsum, erow, aown, ain, anear, jbuf, jflat, amps, crossed, rows_v, flat_v, edge_v, push_v, last_v, resists, band, wanted, factor,
+    sample, gather, fine, coarse, half_last, stack, zbuf, coef, ecoef, passed, rpair, rown, rhalo, rin, rsum, erow, aown, ain, anear, jbuf, jflat, amps, crossed, rows_v, flat_v, edge_v, push_v, last_v, resists, band, wanted, factor,
     load_sem, zs_sem, zr_sem, rs_sem, rr_sem, hs_sem, hr_sem, as_sem, ar_sem, near_sem, pass_sem,
 ):
     t = lax.axis_index("tile")
@@ -350,7 +350,8 @@
         return remote(passed, rin.at[4], hs_sem.at[core], hr_sem.at[1], (bend, 2 * (c - 1) + core))
 
     def part(mask):
-        return remote(rown, rin.at[mask - 1], rs_sem.at[mask - 1], rr_sem.at[mask - 1], partner(mask))
+        source = rown if mask == 1 else rpair
+        return remote(source, rin.at[mask - 1], rs_sem.at[mask - 1], rr_sem.at[mask - 1], partner(mask))
 
     def kernels_to(mask, chunk):
         device = partner(1) if mask != 2 else mirror
@@ -376,11 +377,14 @@
         for side in range(2):
             halo_via(side).start()
 
-    for mask in range(1, GROUP):
-        part(mask).start()
-    for mask in (2, 1):
-        for chunk in range(2):
-            kernels_to(mask, chunk).start()
+    part(1).start()
+    kernels_to(2, 0).start()
+    part(1).wait_recv()
+    rpair[...] = rown[...] + rin[0]
+    part(2).start()
+    kernels_to(2, 1).start()
+    for chunk in range(2):
+        kernels_to(1, chunk).start()
 
     @pl.when(relays)
     def _():
@@ -409,10 +413,9 @@
     def _():
         halo_prev(0).wait_recv()
 
-    for mask in range(1, GROUP):
-        part(mask).wait_recv()
-
-    total = rown[...] + rin[0] + rin[1] + rin[2] + rin[3] + rin[4]
+    part(2).wait_recv()
+
+    total = rpair[...] + rin[1] + rin[3] + rin[4]
     total = total * (1.0 / (SIZE * SIZE))
     keep = row < SPARE
     turn = pltpu.roll(total, FLAT, 1)
@@ -691,7 +694,8 @@
             halo_passed(core).wait_send()
 
     for mask in range(1, GROUP):
-        part(mask).wait_send()
+        if mask < GROUP - 1:
+            part(mask).wait_send()
         for chunk in range(2):
             kernels_to(mask, chunk).wait_send()
         adjoint_part(mask).wait_send()
@@ -735,6 +739,7 @@
             pltpu.VMEM((GROUP, WIRE, VR), F32),
             pltpu.VMEM((GROUP, DEPTH, 4, UH, VR), F32),
             pltpu.VMEM((GROUP, 2, EDGE, VR), F32),
+            pltpu.VMEM((UH, VR), F32),
             pltpu.VMEM((UH, VR), F32),
             pltpu.VMEM((UH, VR), F32),
             pltpu.VMEM((UH, VR), F32),

time: 26.5 us -> 26.1 us (0.985)
  Pallas kernels: 25.7 us -> 25.2 us
    pallas_call x1, Pallas kernels: 25.7 us -> 25.2 us  [shards(): call(*(pltpu.with_memory_space_constraint(x, pltpu.HBM) for x in arrays))]
where the time goes in v13:
time: 26.1 us; the launch traced here: 26 us
  Pallas kernels  25.2 us (97%)
  local copies, waits for them, and re-layouts  0.71 us (3%)
    pallas_call x1, Pallas kernels, shards(): call(*(pltpu.with_memory_space_constraint(x, pltpu.HBM) for x in arrays))  25.2 us
    unnamed x1, local copies, waits for them, and re-layouts  0.71 us

profile of v13, /device:TPU:2, one launch (start us, length us, event | category | flops | bytes accessed | tf_op | source)
XLA Modules:
  0.0 26.0 jit_solution(14935346663750869166)
XLA Ops:
  0.0 25.2 %window_gradient.1 = f32[128,512]{1,0:T(8,128)S(1)} custom-call(f32[128,512]{1,0:T(8,128)} %theta_h.1, s32[512,512]{1,0:T(8,128)} %target_h.1, f32[2,65,2,65]{3,2,1,0:T(2,128)} %bitcast.2, f32[2,65,2,65]{3,2,1,0:T(2,128)} %bitcast.3, s32[8]{0:T(128)} %weights_h.1, f32[2]{0:T(128)} %thresholds_h.1, bf16[512,256]{1,0:T(8,128)(2,1)} %constant.22.clone.by_h, ...), custom_call_target="tpu_custom_call" | custom-call | tf_op jit(solution)/shard_map/window_gradient/pallas_call | solution.py:782
  25.3 0.7 %copy.19 = f32[128,512]{1,0:T(8,128)} copy(f32[128,512]{1,0:T(8,128)S(1)} %window_gradient.1) | data formatting | bytes 524288

commit v14 on v13

--- a/solution.py
+++ b/solution.py
@@ -164,7 +164,7 @@
     sample_h, gather_h, fine_h, coarse_h, half_last_h,
     out_v,
     weights_s, thresholds_s, theta_v, target_v, raw_v, by, bt, pack, turned, pv, pu,
-    sample, gather, fine, coarse, half_last, stack, zbuf, coef, ecoef, passed, rpair, rown, rhalo, rin, rsum, erow, aown, ain, anear, jbuf, jflat, amps, crossed, rows_v, flat_v, edge_v, push_v, last_v, resists, band, wanted, factor,
+    sample, gather, fine, coarse, half_last, stack, zbuf, coef, ecoef, passed, rpair, apair, rown, rhalo, rin, rsum, erow, aown, ain, anear, jbuf, jflat, amps, crossed, rows_v, flat_v, edge_v, push_v, last_v, resists, band, wanted, factor,
     load_sem, zs_sem, zr_sem, rs_sem, rr_sem, hs_sem, hr_sem, as_sem, ar_sem, near_sem, pass_sem,
 ):
     t = lax.axis_index("tile")
@@ -626,7 +626,8 @@
     aown[...] = jnp.where(row == SPARE, jnp.sum(jflat[...], axis=0, keepdims=True), value)
 
     def adjoint_part(mask):
-        return remote(aown, ain.at[mask - 1], as_sem.at[mask - 1], ar_sem.at[mask - 1], partner(mask))
+        source = aown if mask == 1 else apair
+        return remote(source, ain.at[mask - 1], as_sem.at[mask - 1], ar_sem.at[mask - 1], partner(mask))
 
     def adjoint_prev():
         return remote(aown, anear.at[c], as_sem.at[3], near_sem.at[c], (t - 1, GROUP - 1))
@@ -645,8 +646,7 @@
     def _():
         adjoint_next().start()
 
-    for mask in range(1, GROUP):
-        adjoint_part(mask).start()
+    adjoint_part(1).start()
 
     near = (first & has_prev) | (final & has_next)
 
@@ -654,8 +654,10 @@
     for copy in load_bt:
         copy.wait()
 
-    for mask in range(1, GROUP):
-        adjoint_part(mask).wait_recv()
+    adjoint_part(1).wait_recv()
+    apair[...] = aown[...] + ain[0]
+    adjoint_part(2).start()
+    adjoint_part(2).wait_recv()
 
     def sensitivity(value, rows, columns):
         hi, lo = split(jnp.concatenate(unpacked(value), axis=0))
@@ -663,7 +665,7 @@
         hi, lo = split(dot(pack[rows, columns], value))
         return dot(jnp.concatenate([hi, lo, hi], axis=1), bt[...])
 
-    out_v[...] = sensitivity(aown[...] + ain[0] + ain[1] + ain[2], slice(None), slice(0, 256)) * factor[...]
+    out_v[...] = sensitivity(apair[...] + ain[1], slice(None), slice(0, 256)) * factor[...]
 
     @pl.when(near)
     def _():
@@ -696,9 +698,9 @@
     for mask in range(1, GROUP):
         if mask < GROUP - 1:
             part(mask).wait_send()
+            adjoint_part(mask).wait_send()
         for chunk in range(2):
             kernels_to(mask, chunk).wait_send()
-        adjoint_part(mask).wait_send()
 
     @pl.when(has_prev)
     def _():
@@ -739,6 +741,7 @@
             pltpu.VMEM((GROUP, WIRE, VR), F32),
             pltpu.VMEM((GROUP, DEPTH, 4, UH, VR), F32),
             pltpu.VMEM((GROUP, 2, EDGE, VR), F32),
+            pltpu.VMEM((UH, VR), F32),
             pltpu.VMEM((UH, VR), F32),
             pltpu.VMEM((UH, VR), F32),
             pltpu.VMEM((UH, VR), F32),

time: 26.1 us -> 26.1 us (level)
  no operation moved by 1% of the time
where the time goes in v14:
time: 26.1 us; the launch traced here: 26 us
  Pallas kernels  25.2 us (97%)
  local copies, waits for them, and re-layouts  0.71 us (3%)
    pallas_call x1, Pallas kernels, shards(): call(*(pltpu.with_memory_space_constraint(x, pltpu.HBM) for x in arrays))  25.2 us
    unnamed x1, local copies, waits for them, and re-layouts  0.71 us

profile of v14, /device:TPU:2, one launch (start us, length us, event | category | flops | bytes accessed | tf_op | source)
XLA Modules:
  0.0 26.0 jit_solution(10128990610883486711)
XLA Ops:
  0.0 25.2 %window_gradient.1 = f32[128,512]{1,0:T(8,128)S(1)} custom-call(f32[128,512]{1,0:T(8,128)} %theta_h.1, s32[512,512]{1,0:T(8,128)} %target_h.1, f32[2,65,2,65]{3,2,1,0:T(2,128)} %bitcast.2, f32[2,65,2,65]{3,2,1,0:T(2,128)} %bitcast.3, s32[8]{0:T(128)} %weights_h.1, f32[2]{0:T(128)} %thresholds_h.1, bf16[512,256]{1,0:T(8,128)(2,1)} %constant.22.clone.by_h, ...), custom_call_target="tpu_custom_call" | custom-call | tf_op jit(solution)/shard_map/window_gradient/pallas_call | solution.py:785
  25.3 0.7 %copy.19 = f32[128,512]{1,0:T(8,128)} copy(f32[128,512]{1,0:T(8,128)S(1)} %window_gradient.1) | data formatting | bytes 524288

commit v15 on v13

--- a/solution.py
+++ b/solution.py
@@ -379,10 +379,10 @@
 
     part(1).start()
     kernels_to(2, 0).start()
+    kernels_to(2, 1).start()
     part(1).wait_recv()
     rpair[...] = rown[...] + rin[0]
     part(2).start()
-    kernels_to(2, 1).start()
     for chunk in range(2):
         kernels_to(1, chunk).start()
 

time: 26.1 us -> 26 us (level)
  no operation moved by 1% of the time
where the time goes in v15:
time: 26 us; the launch traced here: 25.9 us
  Pallas kernels  25.2 us (97%)
  local copies, waits for them, and re-layouts  0.71 us (3%)
    pallas_call x1, Pallas kernels, shards(): call(*(pltpu.with_memory_space_constraint(x, pltpu.HBM) for x in arrays))  25.2 us
    unnamed x1, local copies, waits for them, and re-layouts  0.71 us

profile of v15, /device:TPU:2, one launch (start us, length us, event | category | flops | bytes accessed | tf_op | source)
XLA Modules:
  0.0 25.9 jit_solution(8125266194882524646)
XLA Ops:
  0.0 25.2 %window_gradient.1 = f32[128,512]{1,0:T(8,128)S(1)} custom-call(f32[128,512]{1,0:T(8,128)} %theta_h.1, s32[512,512]{1,0:T(8,128)} %target_h.1, f32[2,65,2,65]{3,2,1,0:T(2,128)} %bitcast.2, f32[2,65,2,65]{3,2,1,0:T(2,128)} %bitcast.3, s32[8]{0:T(128)} %weights_h.1, f32[2]{0:T(128)} %thresholds_h.1, bf16[512,256]{1,0:T(8,128)(2,1)} %constant.22.clone.by_h, ...), custom_call_target="tpu_custom_call" | custom-call | tf_op jit(solution)/shard_map/window_gradient/pallas_call | solution.py:782
  25.2 0.7 %copy.19 = f32[128,512]{1,0:T(8,128)} copy(f32[128,512]{1,0:T(8,128)S(1)} %window_gradient.1) | data formatting | bytes 524288
